TPU v7x, 128 devices: a whole 4x4x4 slice. The times are simulated.
128 devices in a mesh: row: 8 (over y, x_lo), col: 16 (over z, x_hi, core).
Axes of the slice: x: 4 (x_hi: 2, x_lo: 2; x = x_hi * 2 + x_lo), y: 4, z: 4, core: 2. Of those that a mesh axis runs over, the one named last changes fastest.
Arguments:
- pair: bfloat16 [256, 256, 128], P('row', 'col'), may hold values from -6 to 6
- cotangent: bfloat16 [256, 256, 128], P('row', 'col'), may hold values from -6 to 6
- token_mask: int32 [256], replicated, may hold values 0 or 1
- out_in_proj: bfloat16 [128, 640], replicated, may hold values from -0.5 to 0.5
- out_out_proj: bfloat16 [128, 128], replicated, may hold values from -0.5 to 0.5
- in_in_proj: bfloat16 [128, 640], replicated, may hold values from -0.5 to 0.5
- in_out_proj: bfloat16 [128, 128], replicated, may hold values from -0.5 to 0.5
Outputs:
- updated_pair: bfloat16 [256, 256, 128], P('row', 'col')
- pair_grad: bfloat16 [256, 256, 128], P('row', 'col')
- out_in_grad: float32 [128, 640], replicated
- out_out_grad: float32 [128, 128], replicated
- in_in_grad: float32 [128, 640], replicated
- in_out_grad: float32 [128, 128], replicated
All inputs are finite; a program needn't handle non-finite values.
Results may differ from a plain program's by a relative error of at most 0.012.
Values may be sent and summed in bfloat16 or wider, within the bound.
A program may use at most 128 MiB of HBM per device.

v0:
```python
import jax
import jax.numpy as jnp
from jax import lax
from jax.sharding import PartitionSpec as P

H = 128


EPSILON = 1e-05


def shortened(array):
    return jax.tree.map(lambda a: a.astype(jnp.bfloat16) if a.dtype == jnp.float32 else a, array)


def from_everyone(array, axis):
    copies = jnp.broadcast_to(array, (lax.axis_size(axis), *array.shape))
    return lax.all_to_all(copies, axis, split_axis=0, concat_axis=0, tiled=True)


def in_order(tiles, dim):
    shape = list(tiles.shape[1:])
    shape[dim] *= tiles.shape[0]
    return jnp.moveaxis(tiles, 0, dim).reshape(shape)


def collect(array, axis, dim):
    tiles = from_everyone(array, axis)
    return in_order(tiles, dim)


def normalize(values):
    centre = jnp.mean(values, axis=-1, keepdims=True)
    shifted = values - centre
    spread = jnp.mean(shifted * shifted, axis=-1, keepdims=True)
    return shifted * lax.rsqrt(spread + EPSILON)


def gating(projected, pair_mask):
    left_value = projected[..., :H]
    left_gate = projected[..., H : 2 * H]
    right_value = projected[..., 2 * H : 3 * H]
    right_gate = projected[..., 3 * H : 4 * H]
    left_full = jax.nn.sigmoid(left_gate) * left_value * pair_mask
    right_full = jax.nn.sigmoid(right_gate) * right_value * pair_mask
    return (left_full, right_full, jax.nn.sigmoid(projected[..., 4 * H :]))


def cols_of(tiles):
    return jax.tree.map(
        lambda part, own: part.astype(own.dtype),
        lax.all_gather(shortened(tiles), "col", axis=1, tiled=True),
        tiles,
    )


def rows_of(tiles):
    return jax.tree.map(
        lambda part, own: part.astype(own.dtype),
        jax.tree.map(lambda part: collect(part, "row", 0), shortened(tiles)),
        tiles,
    )


def to_row_blocks(panel):
    return lax.all_to_all(panel, "col", split_axis=0, concat_axis=1, tiled=True)


def to_col_blocks(panel):
    return lax.all_to_all(panel, "row", split_axis=1, concat_axis=0, tiled=True)


def outgoing_sum(left_tile, right_tile):
    row_panels = rows_of((left_tile, right_tile))
    left_panel = cols_of(left_tile)
    right_rows = to_row_blocks(row_panels[1])
    total = jnp.einsum("ikh,jkh->ijh", left_panel, right_rows, preferred_element_type=jnp.float32)
    return (total, row_panels)


def incoming_sum(left_tile, right_tile):
    col_panels = cols_of((left_tile, right_tile))
    right_all = rows_of(right_tile)
    left_cols = to_col_blocks(col_panels[0])
    total = jnp.einsum("kih,kjh->ijh", left_cols, right_all, preferred_element_type=jnp.float32)
    return (total, col_panels)


def outgoing_grads(tri_grad, row_panels):
    grad_cols = cols_of(tri_grad)
    grad_rows = to_col_blocks(grad_cols)
    left_grad = jnp.einsum(
        "ijh,jkh->ikh", grad_cols, row_panels[1], preferred_element_type=jnp.float32
    )
    right_grad = jnp.einsum(
        "ijh,ikh->jkh", grad_rows, row_panels[0], preferred_element_type=jnp.float32
    )
    return (left_grad, right_grad)


def incoming_grads(tri_grad, col_panels):
    grad_rows = rows_of(tri_grad)
    grad_cols = to_row_blocks(grad_rows)
    left_grad = jnp.einsum(
        "ijh,kjh->kih", grad_cols, col_panels[1], preferred_element_type=jnp.float32
    )
    right_grad = jnp.einsum(
        "kih,ijh->kjh", col_panels[0], grad_rows, preferred_element_type=jnp.float32
    )
    return (left_grad, right_grad)


def forward(pair_in, pair_mask, w_in, w_out, outgoing):
    pair_wide = pair_in.astype(jnp.float32)
    normed = normalize(pair_wide).astype(jnp.bfloat16)
    projected = jnp.dot(normed, w_in, preferred_element_type=jnp.float32)
    left_full, right_full, gate = gating(projected, pair_mask)
    left_tile = left_full.astype(jnp.bfloat16)
    right_tile = right_full.astype(jnp.bfloat16)
    if outgoing:
        triangle_sum, panels = outgoing_sum(left_tile, right_tile)
    else:
        triangle_sum, panels = incoming_sum(left_tile, right_tile)
    tri_normed = normalize(triangle_sum).astype(jnp.bfloat16)
    lifted = jnp.dot(tri_normed, w_out, preferred_element_type=jnp.float32)
    result = (pair_wide + gate * lifted).astype(jnp.bfloat16)
    saved = (pair_wide, normed, projected, gate, triangle_sum, tri_normed, lifted, panels)
    return (result, saved)


def backward(cotan, saved, pair_mask, w_in, w_out, outgoing):
    pair_wide, normed, projected, gate, triangle_sum, tri_normed, lifted, panels = saved
    cot_wide = cotan.astype(jnp.float32)
    lift_grad = gate * cot_wide
    gate_grad = lifted * cot_wide
    out_grad = jnp.einsum(
        "ijh,ijc->hc", tri_normed.astype(jnp.float32), lift_grad, precision=lax.Precision.HIGHEST
    )
    normed_tri_grad = jnp.dot(
        lift_grad, w_out.astype(jnp.float32).T, precision=lax.Precision.HIGHEST
    )
    tri_grad = jax.vjp(normalize, triangle_sum)[1](normed_tri_grad)[0].astype(jnp.bfloat16)
    if outgoing:
        left_grad, right_grad = outgoing_grads(tri_grad, panels)
    else:
        left_grad, right_grad = incoming_grads(tri_grad, panels)
    gate_vjp = jax.vjp(lambda values: gating(values, pair_mask), projected)[1]
    proj_grad = gate_vjp((left_grad, right_grad, gate_grad))[0]
    in_grad = jnp.einsum(
        "ijc,ijq->cq", normed.astype(jnp.float32), proj_grad, precision=lax.Precision.HIGHEST
    )
    normed_grad = jnp.dot(proj_grad, w_in.astype(jnp.float32).T, precision=lax.Precision.HIGHEST)
    pair_grad = (cot_wide + jax.vjp(normalize, pair_wide)[1](normed_grad)[0]).astype(jnp.bfloat16)
    return (pair_grad, in_grad, out_grad)


def local(pair, cotangent, token_mask, out_in_proj, out_out_proj, in_in_proj, in_out_proj):
    row_tile = pair.shape[0]
    col_tile = pair.shape[1]
    row_flags = lax.dynamic_slice_in_dim(
        token_mask, lax.axis_index("row") * row_tile, row_tile, 0
    ).astype(jnp.float32)
    col_flags = lax.dynamic_slice_in_dim(
        token_mask, lax.axis_index("col") * col_tile, col_tile, 0
    ).astype(jnp.float32)
    pair_mask = (row_flags[:, None] * col_flags[None, :])[:, :, None]
    middle, saved_out = forward(pair, pair_mask, out_in_proj, out_out_proj, True)
    updated, saved_in = forward(middle, pair_mask, in_in_proj, in_out_proj, False)
    middle_grad, in_in_part, in_out_part = backward(
        cotangent, saved_in, pair_mask, in_in_proj, in_out_proj, False
    )
    pair_grad, out_in_part, out_out_part = backward(
        middle_grad, saved_out, pair_mask, out_in_proj, out_out_proj, True
    )
    totals = lax.psum((out_in_part, out_out_part, in_in_part, in_out_part), ("row", "col"))
    tokens_all = row_tile * lax.axis_size("row")
    return (
        updated,
        pair_grad,
        totals[0] / tokens_all,
        totals[1] / tokens_all,
        totals[2] / tokens_all,
        totals[3] / tokens_all,
    )


def solution(mesh):
    return jax.shard_map(
        local,
        mesh=mesh,
        in_specs=(P("row", "col", None), P("row", "col", None), P(), P(), P(), P(), P()),
        out_specs=(P("row", "col", None), P("row", "col", None), P(), P(), P(), P()),
        check_vma=False,
    )
```

profile of v0, /device:TPU:1, one launch (start us, length us, event | category | flops | bytes accessed | tf_op | source)
XLA Modules:
  0.0 564.3 jit_solution(1086619950908574980)
XLA Ops:
  14.3 22.1 %all_to_all.92 = bf16[8,32,16,128]{3,2,1,0:T(8,128)(2,1)S(1)} all-to-all(bf16[8,32,16,128]{3,2,1,0:T(8,128)(2,1)S(1)} %broadcast_in_dim.24), channel_id=1, replica_groups=mesh['row'=8,'col'=16] {'row'}, dimensions={0} | all-to-all | bytes 2097152 | tf_op jit(solution)/shard_map/all_to_all | solution.py:18
  36.4 31.5 %all_to_all.93 = bf16[256,16,128]{2,1,0:T(8,128)(2,1)S(1)} all-to-all(bf16[256,16,128]{2,1,0:T(8,128)(2,1)S(1)} %bitcast.135), channel_id=1, replica_groups=mesh['row'=8,'col'=16] {'col'}, dimensions={0} | all-to-all | bytes 2097152 | tf_op jit(solution)/shard_map/all_to_all | solution.py:66
  69.1 2.7 copy.220
  72.3 15.3 %copy.221 = bf16[32,256,128]{0,1,2:T(8,128)(2,1)} copy(bf16[32,256,128]{2,1,0:T(8,128)(2,1)} %all-gather.5.cloned.1.call-done) | data formatting | bytes 4194304 | tf_op jit(solution)/shard_map/all_gather | solution.py:52
  87.6 6.0 %bitcast_reduce_fusion.1 = (f32[32,16]{0,1:T(8,128)S(1)}, f32[128,16,32]{2,1,0:T(8,128)}) fusion(bf16[16,256,128]{1,0,2:T(8,128)(2,1)} %copy.220, bf16[32,256,128]{0,1,2:T(8,128)(2,1)} %copy.221), kind=kOutput, calls=%fused_computation.7 | convolution fusion | flops 33619456 | bytes 3409920 | tf_op jit(solution)/shard_map/ikh,jkh->ijh/dot_general | solution.py:77
  93.6 1.7 copy.222
  101.4 4.2 all-to-all-start.2
  105.7 40.1 %all-gather.7.cloned.1.call-done = bf16[32,256,128]{2,1,0:T(8,128)(2,1)} async-done(((bf16[32,16,128]{2,1,0:T(8,128)(2,1)}), bf16[32,256,128]{2,1,0:T(8,128)(2,1)}) %all-gather.7.cloned.1.call-update) | async-done | bytes 2097168 | tf_op jit(solution)/shard_map/all_gather | solution.py:52
  145.8 4.3 copy.231
  150.1 4.4 all-to-all-start.3
  155.2 3.0 copy.234
  158.2 24.5 %all-to-all-done.3 = bf16[32,256,128]{2,0,1:T(8,128)(2,1)} async-done(((bf16[32,256,128]{2,0,1:T(8,128)(2,1)}), bf16[32,256,128]{2,0,1:T(8,128)(2,1)}, u32[]{:S(2)}, u32[]{:S(2)}) %all-to-all-start.3) | async-done | bytes 2097184 | tf_op jit(solution)/shard_map/all_to_all | solution.py:70
  182.6 3.7 copy.233
  186.4 4.9 copy.235
  191.3 3.6 bitcast_reduce_fusion
  194.8 1.7 copy.236
  196.6 2.0 multiply_reduce_fusion.1
  201.9 17.9 %all_to_all.94 = bf16[8,32,16,128]{3,2,1,0:T(8,128)(2,1)} all-to-all(bf16[8,32,16,128]{3,2,1,0:T(8,128)(2,1)S(1)} %broadcast_in_dim.28), channel_id=1, replica_groups=mesh['row'=8,'col'=16] {'row'}, dimensions={0} | all-to-all | bytes 2097152 | tf_op jit(solution)/shard_map/all_to_all | solution.py:18
  219.8 6.1 %all-to-all-start.5 = ((bf16[256,16,128]{2,1,0:T(8,128)(2,1)}), bf16[256,16,128]{2,1,0:T(8,128)(2,1)}, u32[]{:S(2)}, u32[]{:S(2)}) async-start(bf16[256,16,128]{2,1,0:T(8,128)(2,1)} %bitcast.137), calls=%async_computation.5 | async-start | bytes 2097152 | tf_op jit(solution)/shard_map/all_to_all | solution.py:66
  225.9 15.2 %copy.246 = bf16[32,256,128]{0,1,2:T(8,128)(2,1)} copy(bf16[32,256,128]{2,1,0:T(8,128)(2,1)} %all-gather.7.cloned.1.call-done) | data formatting | bytes 4194304 | tf_op jit(solution)/shard_map/all_gather | solution.py:52
  241.2 15.3 %copy.249 = bf16[32,256,128]{0,1,2:T(8,128)(2,1)} copy(bf16[32,256,128]{2,1,0:T(8,128)(2,1)} %all-gather.9.cloned.1.call-done) | data formatting | bytes 4194304 | tf_op jit(solution)/shard_map/all_gather | solution.py:52
  256.5 3.0 copy.245
  259.4 5.9 %fusion.83 = f32[128,16,32]{2,1,0:T(8,128)} fusion(bf16[256,16,128]{0,1,2:T(8,128)(2,1)} %copy.245, bf16[32,256,128]{0,1,2:T(8,128)(2,1)} %copy.246), kind=kOutput, calls=%fused_computation.151 | convolution fusion | flops 33554432 | bytes 3407872 | tf_op jit(solution)/shard_map/kih,ijh->kjh/dot_general | solution.py:107
  265.4 2.3 copy.247
  267.7 2.5 copy.248
  270.2 2.7 copy.250
  272.9 5.9 %fusion.86 = f32[128,32,16]{1,2,0:T(8,128)} fusion(bf16[16,256,128]{1,0,2:T(8,128)(2,1)} %copy.250, bf16[32,256,128]{0,1,2:T(8,128)(2,1)} %copy.249), kind=kOutput, calls=%fused_computation.154 | convolution fusion | flops 33554432 | bytes 3407872 | tf_op jit(solution)/shard_map/ijh,kjh->kih/dot_general | solution.py:104
  278.8 2.4 copy.251
  281.2 2.6 fusion.18
  286.9 2.1 fusion.22
  289.6 2.4 multiply_reduce_fusion
  296.1 1.9 fusion.68
  302.1 2.0 add_convert_fusion
  305.2 4.2 all-to-all-start.6
  309.5 42.8 %all-gather.11.cloned.1.call-done = bf16[32,256,128]{2,1,0:T(8,128)(2,1)} async-done(((bf16[32,16,128]{2,1,0:T(8,128)(2,1)}), bf16[32,256,128]{2,1,0:T(8,128)(2,1)}) %all-gather.11.cloned.1.call-update) | async-done | bytes 2097168 | tf_op jit(solution)/shard_map/all_gather | solution.py:52
  352.3 4.3 copy.260
  356.6 4.3 all-to-all-start.7
  361.2 2.1 copy.266
  363.3 3.1 copy.263
  366.4 2.1 convolution_bitcast_fusion.2
  371.3 15.3 %copy.267 = bf16[32,256,128]{0,1,2:T(8,128)(2,1)} copy(bf16[32,256,128]{2,1,0:T(8,128)(2,1)} %all-gather.11.cloned.1.call-done) | data formatting | bytes 4194304 | tf_op jit(solution)/shard_map/all_gather | solution.py:52
  386.6 4.9 fusion.85
  392.0 3.7 copy.262
  395.7 4.9 copy.264
  400.6 2.6 fusion.84
  408.7 145.6 %all-reduce.13.cloned.1.call-done = (f32[128,640]{1,0:T(8,128)}, f32[128,128]{1,0:T(8,128)}, f32[128,640]{1,0:T(8,128)}, f32[128,128]{1,0:T(8,128)}) async-done(((f32[128,640]{1,0:T(8,128)}, f32[128,128]{1,0:T(8,128)}, f32[128,640]{1,0:T(8,128)}, f32[128,128]{1,0:T(8,128)}), (f32[128,640]{1,0:T(8,128)}, f32[128,128]{1,0:T(8,128)}, f32[128,640]{1,0:T(8,128)}, ...) | async-done | bytes 786448 | tf_op jit(solution)/shard_map/psum | solution.py:175
  554.3 1.5 broadcast_multiply_fusion.2
  555.8 1.9 broadcast_multiply_fusion
  (155 shorter events, 40.9 us)
Async XLA Ops:
  7.2 90.8 %copy-start = (bf16[128,640]{1,0:T(8,128)(2,1)S(1)}, bf16[128,640]{1,0:T(8,128)(2,1)}, u32[]{:S(2)}) copy-start(bf16[128,640]{1,0:T(8,128)(2,1)} %param.12) | copy-start | bytes 491524
  7.2 65.1 %all-gather.5.cloned.1.call-start = ((), (), s32[]{:S(2)}) async-start(), calls=%async_computation.8 | async-start | bytes 2228224 | tf_op jit(solution)/shard_map/all_gather | solution.py:52
  11.2 0.6 copy-start.15
  14.1 131.7 %all-gather.7.cloned.1.call-start = ((), (), s32[]{:S(2)}) async-start(), calls=%async_computation.9 | async-start | bytes 2228224 | tf_op jit(solution)/shard_map/all_gather | solution.py:52
  93.6 2.2 copy-start.2
  93.6 2.2 copy-start.21
  95.7 1.6 copy-start.17
  97.3 0.6 copy-start.18
  98.4 1.1 copy-start.1
  100.3 1.1 copy-start.4
  101.4 48.6 %all-to-all-start.2 = ((bf16[8,32,16,128]{3,2,1,0:T(8,128)(2,1)}), bf16[8,32,16,128]{3,2,1,0:T(8,128)(2,1)}, u32[]{:S(2)}, u32[]{:S(2)}) async-start(bf16[8,32,16,128]{3,2,1,0:T(8,128)(2,1)} %broadcast_in_dim.25), calls=%async_computation.2 | async-start | bytes 2097152 | tf_op jit(solution)/shard_map/all_to_all | solution.py:18
  150.1 32.6 %all-to-all-start.3 = ((bf16[32,256,128]{2,0,1:T(8,128)(2,1)}), bf16[32,256,128]{2,0,1:T(8,128)(2,1)}, u32[]{:S(2)}, u32[]{:S(2)}) async-start(bf16[32,256,128]{2,0,1:T(8,128)(2,1)} %copy.231), calls=%async_computation.3 | async-start | bytes 4194304 | tf_op jit(solution)/shard_map/all_to_all | solution.py:70
  154.4 86.7 %all-gather.9.cloned.1.call-start = ((), (), s32[]{:S(2)}) async-start(), calls=%async_computation.10 | async-start | bytes 2228224 | tf_op jit(solution)/shard_map/all_gather | solution.py:52
  194.8 1.8 copy-start.20
  196.6 84.6 %copy-start.10 = (f32[32,16]{1,0:T(8,128)}, f32[32,16]{1,0:T(8,128)S(1)}, u32[]{:S(2)}) copy-start(f32[32,16]{1,0:T(8,128)S(1)} %copy.238) | copy-start | bytes 6148
  198.9 82.3 %copy-start.12 = (f32[32,16]{1,0:T(8,128)}, f32[32,16]{1,0:T(8,128)S(1)}, u32[]{:S(2)}) copy-start(f32[32,16]{1,0:T(8,128)S(1)} %copy.240) | copy-start | bytes 6148
  219.8 47.9 %all-to-all-start.5 = ((bf16[256,16,128]{2,1,0:T(8,128)(2,1)}), bf16[256,16,128]{2,1,0:T(8,128)(2,1)}, u32[]{:S(2)}, u32[]{:S(2)}) async-start(bf16[256,16,128]{2,1,0:T(8,128)(2,1)} %bitcast.137), calls=%async_computation.5 | async-start | bytes 2097152 | tf_op jit(solution)/shard_map/all_to_all | solution.py:66
  225.9 126.4 %all-gather.11.cloned.1.call-start = ((), (), s32[]{:S(2)}) async-start(), calls=%async_computation.11 | async-start | bytes 2228224 | tf_op jit(solution)/shard_map/all_gather | solution.py:52
  283.7 1.5 copy-start.22
  283.7 1.5 copy-start.24
  283.7 1.5 copy-start.26
  283.8 1.5 copy-start.28
  283.8 1.5 copy-start.30
  283.8 1.5 copy-start.19
  289.0 0.7 copy-start.5
  289.6 14.5 %copy-start.3 = (bf16[32,16,128]{2,1,0:T(8,128)(2,1)S(1)}, bf16[32,16,128]{2,1,0:T(8,128)(2,1)}, u32[]{:S(2)}) copy-start(bf16[32,16,128]{2,1,0:T(8,128)(2,1)} %get-tuple-element.32) | copy-start | bytes 393220
  305.2 51.4 %all-to-all-start.6 = ((bf16[8,32,16,128]{3,2,1,0:T(8,128)(2,1)}), bf16[8,32,16,128]{3,2,1,0:T(8,128)(2,1)}, u32[]{:S(2)}, u32[]{:S(2)}) async-start(bf16[8,32,16,128]{3,2,1,0:T(8,128)(2,1)} %broadcast_in_dim.62), calls=%async_computation.6 | async-start | bytes 2097152 | tf_op jit(solution)/shard_map/all_to_all | solution.py:18
  356.6 35.4 %all-to-all-start.7 = ((bf16[32,256,128]{2,0,1:T(8,128)(2,1)}), bf16[32,256,128]{2,0,1:T(8,128)(2,1)}, u32[]{:S(2)}, u32[]{:S(2)}) async-start(bf16[32,256,128]{2,0,1:T(8,128)(2,1)} %copy.260), calls=%async_computation.7 | async-start | bytes 4194304 | tf_op jit(solution)/shard_map/all_to_all | solution.py:70
  360.9 193.3 %all-reduce.13.cloned.1.call-start = ((), (), s32[]{:S(2)}) async-start(), calls=%async_computation.12 | async-start | bytes 1572864 | tf_op jit(solution)/shard_map/psum | solution.py:175
  363.3 3.1 copy-start.11
  363.3 3.1 copy-start.13
  363.3 3.1 copy-start.14
  366.4 2.1 copy-start.6
  368.5 1.1 copy-start.23
  368.5 1.1 copy-start.25
  368.5 1.1 copy-start.27
  368.5 1.2 copy-start.29
  368.5 1.2 copy-start.31
  403.7 1.0 copy-start.7
  404.6 1.5 copy-start.8
  404.6 1.5 copy-start.9
  406.1 0.9 copy-start.16
Sparse Core Ops, SparseCore 0:
  14.2 58.0 all-gather.4
  100.5 45.2 all-gather.6
  157.6 47.5 all-gather.8
  304.2 48.0 all-gather.10
  407.7 146.5 all-reduce.12
where the time goes:
time: 566 us; the launch traced here: 564 us
  waiting for transfers between devices  254 us (45%)
  local copies, waits for them, and re-layouts  130 us (23%)
  blocking collectives  71.5 us (13%)
  matrix products  47.2 us (8%)
  starting transfers between devices  23.8 us (4%)
  other arithmetic  23.6 us (4%)
  between operations  14.2 us (3%)
    psum x1, waiting for transfers between devices, local(): lax.psum((out_in_part, out_out_part, in_in_part, in_out_part), ('row', 'c...  146 us
    all_gather x4, waiting for transfers between devices, cols_of(): lax.all_gather(shortened(tiles), 'col', axis=1, tiled=True)  83.4 us
    all_gather x6, local copies, waits for them, and re-layouts, cols_of(): lax.all_gather(shortened(tiles), 'col', axis=1, tiled=True)  69.7 us
    all_to_all x2, blocking collectives, from_everyone(): return lax.all_to_all(copies, axis, split_axis=0, concat_axis=0, tiled=True)  40 us
    all_to_all x1, blocking collectives, to_row_blocks(): return lax.all_to_all(panel, 'col', split_axis=0, concat_axis=1, tiled=True)  31.5 us
    all_to_all x2, waiting for transfers between devices, to_col_blocks(): return lax.all_to_all(panel, 'row', split_axis=1, concat_axis=0, tiled=True)  24.5 us
    all_to_all x4, local copies, waits for them, and re-layouts, to_col_blocks(): return lax.all_to_all(panel, 'row', split_axis=1, concat_axis=0, tiled=True)  17.2 us
  transfers between devices with their start and end apart: 10, of which 5 were waited for; matrix products, arithmetic and copies ran while one was open for 20% of the time, Pallas kernels for 0%

commit v1 on v0

--- a/solution.py
+++ b/solution.py
@@ -1,7 +1,12 @@
 import jax
 import jax.numpy as jnp
 from jax import lax
+from jax.experimental import pallas as pl
+from jax.experimental.pallas import tpu as pltpu
 from jax.sharding import PartitionSpec as P
+
+MESH = pl.DeviceIdType.MESH
+N = 128
 
 H = 128
 
@@ -154,6 +159,78 @@
     return (pair_grad, in_grad, out_grad)
 
 
+def reduce_kernel(x_ref, o_ref, got, total, ssem, rsem):
+    cols = lax.axis_size("col")
+    me = lax.axis_index("row") * cols + lax.axis_index("col")
+
+    def peer(step):
+        other = lax.rem(me + step, N)
+        return (other // cols, lax.rem(other, cols))
+
+    bar = pltpu.get_barrier_semaphore()
+
+    @pl.loop(1, N)
+    def _(step):
+        pl.semaphore_signal(bar, inc=1, device_id=peer(step), device_id_type=MESH)
+
+    pl.semaphore_wait(bar, N - 1)
+
+    def await_all(ref, sem):
+        part = ref.at[pl.ds(0, N - 1)]
+        pltpu.make_async_copy(part, part, sem).wait()
+
+    @pl.loop(1, N)
+    def _(step):
+        a, b = peer(step)
+        pltpu.make_async_remote_copy(
+            src_ref=x_ref.at[a * cols + b], dst_ref=got.at[me], send_sem=ssem.at[0],
+            recv_sem=rsem.at[0], device_id=(a, b), device_id_type=MESH,
+        ).start()
+
+    got[me] = x_ref[me]
+    await_all(got, rsem.at[0])
+    total[...] = jnp.sum(got[...].astype(jnp.float32), axis=0).astype(jnp.bfloat16)
+
+    @pl.loop(1, N)
+    def _(step):
+        pltpu.make_async_remote_copy(
+            src_ref=total, dst_ref=o_ref.at[me], send_sem=ssem.at[1],
+            recv_sem=rsem.at[1], device_id=peer(step), device_id_type=MESH,
+        ).start()
+
+    o_ref[me] = total[...]
+    await_all(got, ssem.at[0])
+    await_all(o_ref, rsem.at[1])
+    await_all(o_ref, ssem.at[1])
+
+
+def reduce_all(parts):
+    flat = jnp.concatenate([part.reshape(-1, 128) for part in parts], axis=0)
+    tiles = flat.reshape(N, -1, 128)
+    rows = tiles.shape[1]
+    tiles = jnp.pad(tiles, ((0, 0), (0, 16 - rows), (0, 0))).astype(jnp.bfloat16)
+    out = pl.pallas_call(
+        reduce_kernel,
+        out_shape=jax.ShapeDtypeStruct(tiles.shape, jnp.bfloat16),
+        in_specs=[pl.BlockSpec(memory_space=pltpu.VMEM)],
+        out_specs=pl.BlockSpec(memory_space=pltpu.VMEM),
+        scratch_shapes=[
+            pltpu.VMEM(tiles.shape, jnp.bfloat16),
+            pltpu.VMEM(tiles.shape[1:], jnp.bfloat16),
+            pltpu.SemaphoreType.DMA((2,)),
+            pltpu.SemaphoreType.DMA((2,)),
+        ],
+        compiler_params=pltpu.CompilerParams(collective_id=0, has_side_effects=True),
+    )(tiles)
+    flat = out[:, :rows].astype(jnp.float32).reshape(-1, 128)
+    totals, at = [], 0
+    for part in parts:
+        size = part.size // 128
+        totals.append(flat[at : at + size].reshape(part.shape))
+        at += size
+    return totals
+
+
 def local(pair, cotangent, token_mask, out_in_proj, out_out_proj, in_in_proj, in_out_proj):
     row_tile = pair.shape[0]
     col_tile = pair.shape[1]
@@ -172,7 +249,7 @@
     pair_grad, out_in_part, out_out_part = backward(
         middle_grad, saved_out, pair_mask, out_in_proj, out_out_proj, True
     )
-    totals = lax.psum((out_in_part, out_out_part, in_in_part, in_out_part), ("row", "col"))
+    totals = reduce_all((out_in_part, out_out_part, in_in_part, in_out_part))
     tokens_all = row_tile * lax.axis_size("row")
     return (
         updated,

time: 566 us -> 465 us (0.82)
  waiting for transfers between devices: 254 us -> 108 us
  Pallas kernels: 0 us -> 28.5 us
  starting transfers between devices: 23.8 us -> 32.4 us
  local copies, waits for them, and re-layouts: 130 us -> 136 us
    psum x1 -> x0, waiting for transfers between devices: 146 us -> none  [local(): lax.psum((out_in_part, out_out_part, in_in_part, in_out_part), ('row', 'c...]
    pallas_call x0 -> x1, Pallas kernels: none -> 28.5 us  [reduce_all(): pl.pallas_call(reduce_kernel, out_shape=jax.ShapeDtypeStruct(tiles.shape,...]
    all_to_all x2, starting transfers between devices: 8.7 us -> 17.4 us  [to_col_blocks(): return lax.all_to_all(panel, 'row', split_axis=1, concat_axis=0, tiled=True)]
  transfers between devices with their start and end apart: 10 -> 9, of which waited for: 5 -> 4; matrix products, arithmetic and copies ran while one was open for 20% -> 24% of each run, Pallas kernels for 0% -> 0%
where the time goes in v1:
time: 465 us; the launch traced here: 461 us
  local copies, waits for them, and re-layouts  136 us (29%)
  waiting for transfers between devices  108 us (23%)
  blocking collectives  71.5 us (15%)
  matrix products  45.5 us (10%)
  starting transfers between devices  32.4 us (7%)
  Pallas kernels  28.5 us (6%)
  other arithmetic  23.8 us (5%)
  between operations  14.6 us (3%)
    all_gather x4, waiting for transfers between devices, cols_of(): lax.all_gather(shortened(tiles), 'col', axis=1, tiled=True)  83.5 us
    all_gather x6, local copies, waits for them, and re-layouts, cols_of(): lax.all_gather(shortened(tiles), 'col', axis=1, tiled=True)  69.4 us
    all_to_all x2, blocking collectives, from_everyone(): return lax.all_to_all(copies, axis, split_axis=0, concat_axis=0, tiled=True)  40 us
    all_to_all x1, blocking collectives, to_row_blocks(): return lax.all_to_all(panel, 'col', split_axis=0, concat_axis=1, tiled=True)  31.5 us
    pallas_call x1, Pallas kernels, reduce_all(): pl.pallas_call(reduce_kernel, out_shape=jax.ShapeDtypeStruct(tiles.shape,...  28.5 us
    all_to_all x2, waiting for transfers between devices, to_col_blocks(): return lax.all_to_all(panel, 'row', split_axis=1, concat_axis=0, tiled=True)  24.4 us
    all_to_all x2, starting transfers between devices, to_col_blocks(): return lax.all_to_all(panel, 'row', split_axis=1, concat_axis=0, tiled=True)  17.4 us
    all_to_all x4, local copies, waits for them, and re-layouts, to_col_blocks(): return lax.all_to_all(panel, 'row', split_axis=1, concat_axis=0, tiled=True)  17.3 us
  transfers between devices with their start and end apart: 9, of which 4 were waited for; matrix products, arithmetic and copies ran while one was open for 24% of the time, Pallas kernels for 0%

profile of v1, /device:TPU:1, one launch (start us, length us, event | category | flops | bytes accessed | tf_op | source)
XLA Modules:
  0.0 460.7 jit_solution(9489504931164446457)
XLA Ops:
  14.3 22.1 %all_to_all.92 = bf16[8,32,16,128]{3,2,1,0:T(8,128)(2,1)S(1)} all-to-all(bf16[8,32,16,128]{3,2,1,0:T(8,128)(2,1)S(1)} %broadcast_in_dim.24), channel_id=1, replica_groups=mesh['row'=8,'col'=16] {'row'}, dimensions={0} | all-to-all | bytes 2097152 | tf_op jit(solution)/shard_map/all_to_all | solution.py:23
  36.4 31.5 %all_to_all.93 = bf16[256,16,128]{2,1,0:T(8,128)(2,1)S(1)} all-to-all(bf16[256,16,128]{2,1,0:T(8,128)(2,1)S(1)} %bitcast.143), channel_id=1, replica_groups=mesh['row'=8,'col'=16] {'col'}, dimensions={0} | all-to-all | bytes 2097152 | tf_op jit(solution)/shard_map/all_to_all | solution.py:71
  69.1 2.7 copy.220
  72.3 15.2 %copy.221 = bf16[32,256,128]{0,1,2:T(8,128)(2,1)} copy(bf16[32,256,128]{2,1,0:T(8,128)(2,1)} %all-gather.5.cloned.1.call-done) | data formatting | bytes 4194304 | tf_op jit(solution)/shard_map/all_gather | solution.py:57
  87.5 6.0 %bitcast_reduce_fusion.1 = (f32[32,16]{0,1:T(8,128)S(1)}, f32[128,16,32]{2,1,0:T(8,128)}) fusion(bf16[16,256,128]{1,0,2:T(8,128)(2,1)} %copy.220, bf16[32,256,128]{0,1,2:T(8,128)(2,1)} %copy.221), kind=kOutput, calls=%fused_computation.11 | convolution fusion | flops 33619456 | bytes 3409920 | tf_op jit(solution)/shard_map/ikh,jkh->ijh/dot_general | solution.py:82
  93.5 1.7 copy.222
  101.3 4.3 all-to-all-start.2
  105.6 40.1 %all-gather.7.cloned.1.call-done = bf16[32,256,128]{2,1,0:T(8,128)(2,1)} async-done(((bf16[32,16,128]{2,1,0:T(8,128)(2,1)}), bf16[32,256,128]{2,1,0:T(8,128)(2,1)}) %all-gather.7.cloned.1.call-update) | async-done | bytes 2097168 | tf_op jit(solution)/shard_map/all_gather | solution.py:57
  145.7 4.3 copy.231
  150.0 4.3 all-to-all-start.3
  155.1 3.0 copy.234
  158.1 24.4 %all-to-all-done.3 = bf16[32,256,128]{2,0,1:T(8,128)(2,1)} async-done(((bf16[32,256,128]{2,0,1:T(8,128)(2,1)}), bf16[32,256,128]{2,0,1:T(8,128)(2,1)}, u32[]{:S(2)}, u32[]{:S(2)}) %all-to-all-start.3) | async-done | bytes 2097184 | tf_op jit(solution)/shard_map/all_to_all | solution.py:75
  182.5 3.8 copy.233
  186.3 4.9 %copy.235 = bf16[256,32,128]{0,1,2:T(8,128)(2,1)} copy(bf16[256,32,128]{2,1,0:T(8,128)(2,1)} %bitcast.147) | data formatting | bytes 4194304 | tf_op jit(solution)/shard_map/all_to_all | solution.py:75
  191.2 3.6 bitcast_reduce_fusion
  194.8 1.7 copy.236
  196.6 2.0 multiply_reduce_fusion.1
  201.8 17.9 %all_to_all.94 = bf16[8,32,16,128]{3,2,1,0:T(8,128)(2,1)} all-to-all(bf16[8,32,16,128]{3,2,1,0:T(8,128)(2,1)S(1)} %broadcast_in_dim.28), channel_id=1, replica_groups=mesh['row'=8,'col'=16] {'row'}, dimensions={0} | all-to-all | bytes 2097152 | tf_op jit(solution)/shard_map/all_to_all | solution.py:23
  219.8 6.1 %all-to-all-start.5 = ((bf16[256,16,128]{2,1,0:T(8,128)(2,1)}), bf16[256,16,128]{2,1,0:T(8,128)(2,1)}, u32[]{:S(2)}, u32[]{:S(2)}) async-start(bf16[256,16,128]{2,1,0:T(8,128)(2,1)} %bitcast.145), calls=%async_computation.5 | async-start | bytes 2097152 | tf_op jit(solution)/shard_map/all_to_all | solution.py:71
  225.9 15.2 %copy.246 = bf16[32,256,128]{0,1,2:T(8,128)(2,1)} copy(bf16[32,256,128]{2,1,0:T(8,128)(2,1)} %all-gather.7.cloned.1.call-done) | data formatting | bytes 4194304 | tf_op jit(solution)/shard_map/all_gather | solution.py:57
  241.1 15.2 %copy.249 = bf16[32,256,128]{0,1,2:T(8,128)(2,1)} copy(bf16[32,256,128]{2,1,0:T(8,128)(2,1)} %all-gather.9.cloned.1.call-done) | data formatting | bytes 4194304 | tf_op jit(solution)/shard_map/all_gather | solution.py:57
  256.3 3.0 copy.245
  259.4 5.9 %fusion.87 = f32[128,16,32]{2,1,0:T(8,128)} fusion(bf16[256,16,128]{0,1,2:T(8,128)(2,1)} %copy.245, bf16[32,256,128]{0,1,2:T(8,128)(2,1)} %copy.246), kind=kOutput, calls=%fused_computation.157 | convolution fusion | flops 33554432 | bytes 3407872 | tf_op jit(solution)/shard_map/kih,ijh->kjh/dot_general | solution.py:112
  265.2 2.3 copy.247
  267.6 2.5 copy.248
  270.1 2.7 copy.250
  272.7 5.9 %fusion.90 = f32[128,32,16]{1,2,0:T(8,128)} fusion(bf16[16,256,128]{1,0,2:T(8,128)(2,1)} %copy.250, bf16[32,256,128]{0,1,2:T(8,128)(2,1)} %copy.249), kind=kOutput, calls=%fused_computation.160 | convolution fusion | flops 33554432 | bytes 3407872 | tf_op jit(solution)/shard_map/ijh,kjh->kih/dot_general | solution.py:109
  278.7 2.4 copy.251
  281.0 2.6 fusion.22
  283.7 2.0 fusion.20
  287.9 1.9 fusion.59
  293.9 2.1 fusion.26
  296.6 1.6 multiply_reduce_fusion
  300.4 1.9 fusion.72
  306.4 2.0 add_convert_fusion
  309.5 4.2 all-to-all-start.6
  313.8 42.8 %all-gather.11.cloned.1.call-done = bf16[32,256,128]{2,1,0:T(8,128)(2,1)} async-done(((bf16[32,16,128]{2,1,0:T(8,128)(2,1)}), bf16[32,256,128]{2,1,0:T(8,128)(2,1)}) %all-gather.11.cloned.1.call-update) | async-done | bytes 2097168 | tf_op jit(solution)/shard_map/all_gather | solution.py:57
  356.6 4.3 copy.260
  360.9 13.1 %all-to-all-start.7 = ((bf16[32,256,128]{2,0,1:T(8,128)(2,1)}), bf16[32,256,128]{2,0,1:T(8,128)(2,1)}, u32[]{:S(2)}, u32[]{:S(2)}) async-start(bf16[32,256,128]{2,0,1:T(8,128)(2,1)} %copy.260), calls=%async_computation.7 | async-start | bytes 4194304 | tf_op jit(solution)/shard_map/all_to_all | solution.py:75
  373.9 2.1 copy.266
  376.0 3.0 copy.263
  379.1 2.1 fusion.3
  383.3 15.2 %copy.267 = bf16[32,256,128]{0,1,2:T(8,128)(2,1)} copy(bf16[32,256,128]{2,1,0:T(8,128)(2,1)} %all-gather.11.cloned.1.call-done) | data formatting | bytes 4194304 | tf_op jit(solution)/shard_map/all_gather | solution.py:57
  398.5 4.9 %fusion.89 = f32[128,16,32]{2,1,0:T(8,128)S(1)} fusion(bf16[256,16,128]{0,1,2:T(8,128)(2,1)} %copy.266, bf16[32,256,128]{0,1,2:T(8,128)(2,1)} %copy.267), kind=kOutput, calls=%fused_computation.159 | convolution fusion | flops 33554432 | bytes 3407872 | tf_op jit(solution)/shard_map/ijh,jkh->ikh/dot_general | solution.py:97
  404.0 3.8 copy.262
  407.7 4.9 %copy.264 = bf16[256,32,128]{0,1,2:T(8,128)(2,1)} copy(bf16[256,32,128]{2,1,0:T(8,128)(2,1)} %bitcast.148) | data formatting | bytes 4194304 | tf_op jit(solution)/shard_map/all_to_all | solution.py:75
  412.6 2.6 fusion.88
  418.9 28.5 %shard_map.118 = bf16[128,16,128]{2,1,0:T(8,128)(2,1)} custom-call(bf16[128,16,128]{2,1,0:T(8,128)(2,1)} %pad.45.x_ref), custom_call_target="tpu_custom_call" | custom-call | tf_op jit(solution)/shard_map/pallas_call | solution.py:212
  (196 shorter events, 45.9 us)
Async XLA Ops:
  7.2 90.7 %copy-start = (bf16[128,640]{1,0:T(8,128)(2,1)S(1)}, bf16[128,640]{1,0:T(8,128)(2,1)}, u32[]{:S(2)}) copy-start(bf16[128,640]{1,0:T(8,128)(2,1)} %param.12) | copy-start | bytes 491524
  7.2 65.1 %all-gather.5.cloned.1.call-start = ((), (), s32[]{:S(2)}) async-start(), calls=%async_computation.8 | async-start | bytes 2228224 | tf_op jit(solution)/shard_map/all_gather | solution.py:57
  11.9 269.2 %copy-start.17 = (f32[32,16]{1,0:T(8,128)}, f32[32,16]{1,0:T(8,128)S(1)}, u32[]{:S(2)}) copy-start(f32[32,16]{1,0:T(8,128)S(1)} %broadcast_multiply_fusion) | copy-start | bytes 6148
  14.1 131.5 %all-gather.7.cloned.1.call-start = ((), (), s32[]{:S(2)}) async-start(), calls=%async_computation.9 | async-start | bytes 2228224 | tf_op jit(solution)/shard_map/all_gather | solution.py:57
  93.5 2.2 copy-start.2
  93.5 2.2 copy-start.37
  95.6 1.6 copy-start.30
  95.7 210.7 %copy-start.20 = (f32[32,16]{1,0:T(8,128)}, f32[32,16]{1,0:T(8,128)S(1)}, u32[]{:S(2)}) copy-start(f32[32,16]{1,0:T(8,128)S(1)} %copy.226) | copy-start | bytes 6148
  98.3 1.1 copy-start.1
  100.2 1.1 copy-start.4
  101.3 48.7 %all-to-all-start.2 = ((bf16[8,32,16,128]{3,2,1,0:T(8,128)(2,1)}), bf16[8,32,16,128]{3,2,1,0:T(8,128)(2,1)}, u32[]{:S(2)}, u32[]{:S(2)}) async-start(bf16[8,32,16,128]{3,2,1,0:T(8,128)(2,1)} %broadcast_in_dim.25), calls=%async_computation.2 | async-start | bytes 2097152 | tf_op jit(solution)/shard_map/all_to_all | solution.py:23
  150.0 32.6 %all-to-all-start.3 = ((bf16[32,256,128]{2,0,1:T(8,128)(2,1)}), bf16[32,256,128]{2,0,1:T(8,128)(2,1)}, u32[]{:S(2)}, u32[]{:S(2)}) async-start(bf16[32,256,128]{2,0,1:T(8,128)(2,1)} %copy.231), calls=%async_computation.3 | async-start | bytes 4194304 | tf_op jit(solution)/shard_map/all_to_all | solution.py:75
  154.3 86.8 %all-gather.9.cloned.1.call-start = ((), (), s32[]{:S(2)}) async-start(), calls=%async_computation.10 | async-start | bytes 2228224 | tf_op jit(solution)/shard_map/all_gather | solution.py:57
  194.8 1.8 copy-start.36
  196.6 84.5 %copy-start.22 = (f32[32,16]{1,0:T(8,128)}, f32[32,16]{1,0:T(8,128)S(1)}, u32[]{:S(2)}) copy-start(f32[32,16]{1,0:T(8,128)S(1)} %copy.238) | copy-start | bytes 6148
  198.9 82.2 %copy-start.24 = (f32[32,16]{1,0:T(8,128)}, f32[32,16]{1,0:T(8,128)S(1)}, u32[]{:S(2)}) copy-start(f32[32,16]{1,0:T(8,128)S(1)} %copy.240) | copy-start | bytes 6148
  219.8 47.8 %all-to-all-start.5 = ((bf16[256,16,128]{2,1,0:T(8,128)(2,1)}), bf16[256,16,128]{2,1,0:T(8,128)(2,1)}, u32[]{:S(2)}, u32[]{:S(2)}) async-start(bf16[256,16,128]{2,1,0:T(8,128)(2,1)} %bitcast.145), calls=%async_computation.5 | async-start | bytes 2097152 | tf_op jit(solution)/shard_map/all_to_all | solution.py:71
  225.8 130.8 %all-gather.11.cloned.1.call-start = ((), (), s32[]{:S(2)}) async-start(), calls=%async_computation.11 | async-start | bytes 2228224 | tf_op jit(solution)/shard_map/all_gather | solution.py:57
  283.6 2.1 copy-start.39
  283.6 2.1 copy-start.41
  283.6 2.1 copy-start.43
  283.6 2.1 copy-start.45
  283.6 2.1 copy-start.47
  283.6 2.9 copy-start.33
  283.6 10.2 %copy-start.26 = (bf16[32,16,128]{2,1,0:T(8,128)(2,1)S(1)}, bf16[32,16,128]{2,1,0:T(8,128)(2,1)}, u32[]{:S(2)}) copy-start(bf16[32,16,128]{2,1,0:T(8,128)(2,1)} %param.8) | copy-start | bytes 393220
  293.9 2.8 copy-start.38
  296.0 3.1 copy-start.31
  296.6 11.8 %copy-start.3 = (bf16[32,16,128]{2,1,0:T(8,128)(2,1)S(1)}, bf16[32,16,128]{2,1,0:T(8,128)(2,1)}, u32[]{:S(2)}) copy-start(bf16[32,16,128]{2,1,0:T(8,128)(2,1)} %get-tuple-element.28) | copy-start | bytes 393220
  309.5 51.3 %all-to-all-start.6 = ((bf16[8,32,16,128]{3,2,1,0:T(8,128)(2,1)}), bf16[8,32,16,128]{3,2,1,0:T(8,128)(2,1)}, u32[]{:S(2)}, u32[]{:S(2)}) async-start(bf16[8,32,16,128]{3,2,1,0:T(8,128)(2,1)} %broadcast_in_dim.62), calls=%async_computation.6 | async-start | bytes 2097152 | tf_op jit(solution)/shard_map/all_to_all | solution.py:23
  360.9 43.1 %all-to-all-start.7 = ((bf16[32,256,128]{2,0,1:T(8,128)(2,1)}), bf16[32,256,128]{2,0,1:T(8,128)(2,1)}, u32[]{:S(2)}, u32[]{:S(2)}) async-start(bf16[32,256,128]{2,0,1:T(8,128)(2,1)} %copy.260), calls=%async_computation.7 | async-start | bytes 4194304 | tf_op jit(solution)/shard_map/all_to_all | solution.py:75
  376.0 3.0 copy-start.23
  376.0 3.0 copy-start.25
  376.0 3.0 copy-start.27
  379.1 2.2 copy-start.40
  379.1 2.2 copy-start.42
  379.1 2.2 copy-start.44
  379.1 2.2 copy-start.46
  379.1 2.2 copy-start.48
  416.1 1.5 copy-start.7
  416.2 1.5 copy-start.9
  416.2 1.5 copy-start.11
  416.2 1.5 copy-start.13
  448.5 1.0 copy-start.19
  448.6 1.1 copy-start.10
  448.6 1.2 copy-start.12
  448.6 1.2 copy-start.14
  448.6 1.3 copy-start.16
  450.7 1.7 copy-start.29
  (10 other events, 8.3 us)
Sparse Core Ops, SparseCore 0:
  14.2 58.0 all-gather.4
  100.3 45.2 all-gather.6
  157.5 47.5 all-gather.8
  308.5 48.0 all-gather.10

commit v2 on v0

v2 whole, which is shorter than its diff:
```python
import jax
import jax.numpy as jnp
from jax import lax
from jax.experimental import pallas as pl
from jax.experimental.pallas import tpu as pltpu
from jax.sharding import PartitionSpec as P

MESH = pl.DeviceIdType.MESH
F32 = jnp.float32
BF16 = jnp.bfloat16
EPSILON = 1e-05
N = 128
H = 128
ROWS, COLS = 32, 16
CHUNKS = 4
TOKENS = 256
OUT_LR, OUT_TRI, IN_LR, IN_TRI, IN_BACK, IN_SIDES, OUT_BACK, OUT_SIDES = range(8)
IN_SUM, IN_SHARE, OUT_SUM, OUT_SHARE = range(8, 12)
EXCHANGES = 12


def nn(a, b):
    return lax.dot_general(a, b, (((1,), (0,)), ((), ())), preferred_element_type=F32)


def nt(a, b):
    return lax.dot_general(a, b, (((1,), (1,)), ((), ())), preferred_element_type=F32)


def tn(a, b):
    return lax.dot_general(a, b, (((0,), (0,)), ((), ())), preferred_element_type=F32)


def token_rows(x):
    return [8 * hi + 4 * b + x for b in range(2) for hi in range(4)]


def at(x):
    return slice(128 * x, 128 * (x + 1))


def norm(v):
    shifted = v - jnp.mean(v, axis=0, keepdims=True)
    inv = lax.rsqrt(jnp.mean(shifted * shifted, axis=0, keepdims=True) + EPSILON)
    return shifted * inv, inv


def norm_grad(dy, y, inv):
    return inv * (
        dy - jnp.mean(dy, axis=0, keepdims=True) - y * jnp.mean(dy * y, axis=0, keepdims=True)
    )


def halves(a, b):
    low = lax.broadcasted_iota(jnp.int32, a.shape, 1) < 64
    return jnp.where(low, a, pltpu.roll(b, 64, 1)), jnp.where(low, pltpu.roll(a, 64, 1), b)


def interchange(v):
    v = list(v)
    lane = lax.broadcasted_iota(jnp.int32, v[0].shape, 1)
    for bit in range(3):
        step = 16 << bit
        low = (lane & step) == 0
        for u in range(8):
            w = u | (1 << bit)
            if w == u:
                continue
            a, b = v[u], v[w]
            v[u] = jnp.where(low, a, pltpu.roll(b, step, 1))
            v[w] = jnp.where(low, pltpu.roll(a, 128 - step, 1), b)
    return v


def kernel(
    pair_ref, cot_ref, flags_ref, wio_ref, woo_ref, wii_ref, woi_ref,
    upd_ref, pg_ref, gio_ref, goo_ref, gii_ref, goi_ref,
    send, got, share, wide, mats, tall, mask_ref,
    z_ref, y_ref, yinv_ref, n_ref, proj_ref, gate_ref, t_ref, tinv_ref, tn_ref, lifted_ref,
    sides_ref, res_ref, lg_ref, pgr_ref, wint_ref, woutt_ref,
    ssem, rsem,
):
    cols = lax.axis_size("col")
    row, col = lax.axis_index("row"), lax.axis_index("col")
    me = row * cols + col

    def peer(step):
        other = lax.rem(me + step, N)
        return other // cols, lax.rem(other, cols)

    bar = pltpu.get_barrier_semaphore()

    @pl.loop(1, N)
    def _(step):
        pl.semaphore_signal(bar, inc=1, device_id=peer(step), device_id_type=MESH)

    def start(k):
        @pl.loop(1, N)
        def _(step):
            a, b = peer(step)
            pltpu.make_async_remote_copy(
                src_ref=send.at[k, a * cols + b], dst_ref=got.at[k, me], send_sem=ssem.at[k],
                recv_sem=rsem.at[k], device_id=(a, b), device_id_type=MESH,
            ).start()

        got[k, me] = send[k, me]

    def start_share(k, s):
        @pl.loop(1, N)
        def _(step):
            pltpu.make_async_remote_copy(
                src_ref=share.at[s], dst_ref=got.at[k, me], send_sem=ssem.at[k],
                recv_sem=rsem.at[k], device_id=peer(step), device_id_type=MESH,
            ).start()

        got[k, me] = share[s]

    def await_all(k, sem):
        part = got.at[k, pl.ds(0, N - 1)]
        pltpu.make_async_copy(part, part, sem.at[k]).wait()

    def put_pair(x, left, right):
        first, second = halves(left, right)
        wide[pl.ds(x, H, stride=8), :] = first
        wide[pl.ds(4 + x, H, stride=8), :] = second

    def pack(k):
        send[k] = wide[...].reshape(N, 8, 128).astype(BF16)

    def unpack(k):
        wide[...] = got[k].astype(F32).reshape(N * 8, 128)

    def take_pair(x):
        return halves(wide[pl.ds(x, H, stride=8), :], wide[pl.ds(4 + x, H, stride=8), :])

    def assemble(k):
        @pl.loop(0, 8)
        def _(r):
            for hi in range(2):
                v = interchange([got[k, r * 16 + hi * 8 + lo].astype(F32) for lo in range(8)])
                for t in range(2):
                    for ih in range(4):
                        rows = pl.ds(pl.multiple_of(r * 32 + ih * 8, 8), 8)
                        tall[t, rows, at(hi)] = v[t * 4 + ih]

    def disperse(k):
        @pl.loop(0, 8)
        def _(r):
            for hi in range(2):
                v = interchange([
                    tall[t, pl.ds(pl.multiple_of(r * 32 + ih * 8, 8), 8), at(hi)]
                    for t in range(2) for ih in range(4)
                ])
                for lo in range(8):
                    send[k, r * 16 + hi * 8 + lo] = v[lo].astype(BF16)

    def set_weights(w_in_ref, w_out_ref, s):
        wint_ref[s] = w_in_ref[...].astype(F32).T.astype(BF16)
        woutt_ref[s] = w_out_ref[...].astype(F32).T.astype(BF16)

    def project(s, k):
        for x in range(CHUNKS):
            y, inv = norm(z_ref[s, :, at(x)])
            y_ref[s, :, at(x)] = y
            yinv_ref[s, :, at(x)] = inv
            normed = y.astype(BF16)
            n_ref[s, :, at(x)] = normed
            mask = mask_ref[0:1, at(x)]
            p = nn(wint_ref[s], normed)
            proj_ref[s, :, at(x)] = p
            left = jax.nn.sigmoid(p[H : 2 * H]) * p[:H] * mask
            right = jax.nn.sigmoid(p[3 * H : 4 * H]) * p[2 * H : 3 * H] * mask
            put_pair(x, left, right)
        pack(k)
        start(k)
        gate_ref[s] = jax.nn.sigmoid(proj_ref[s, 4 * H :, :])

    def multiply(s, k_in, k_out, outgoing):
        await_all(k_in, rsem)
        assemble(k_in)
        mats[s] = tall[...].astype(BF16)
        if outgoing:
            tri = nt(mats[s, 0], mats[s, 1])
        else:
            tri = tn(mats[s, 0], mats[s, 1])
        high = tri.astype(BF16).astype(F32)
        tall[0] = high
        tall[1] = tri - high
        disperse(k_out)
        start(k_out)

    def lift(s, k, keep):
        await_all(k, rsem)
        unpack(k)
        for x in range(CHUNKS):
            high, low = take_pair(x)
            y, inv = norm(high + low)
            t_ref[s, :, at(x)] = y
            tinv_ref[s, :, at(x)] = inv
            normed = y.astype(BF16)
            tn_ref[s, :, at(x)] = normed
            lifted = nn(woutt_ref[s], normed)
            lifted_ref[s, :, at(x)] = lifted
            keep(x, (z_ref[s, :, at(x)] + gate_ref[s, :, at(x)] * lifted).astype(BF16))

    def back(s, w_out_ref, k):
        for x in range(CHUNKS):
            dres = res_ref[s, :, at(x)]
            lift_grad = (gate_ref[s, :, at(x)] * dres).astype(BF16)
            lg_ref[:, at(x)] = lift_grad
            dy = nn(w_out_ref[...], lift_grad)
            tri_grad = norm_grad(dy, t_ref[s, :, at(x)], tinv_ref[s, :, at(x)])
            put_pair(x, tri_grad, jnp.zeros_like(tri_grad))
        pack(k)
        start(k)

    def side_products(s, k_in, k_out, outgoing):
        await_all(k_in, rsem)
        assemble(k_in)
        grad = tall[0].astype(BF16)
        left, right = mats[s, 0], mats[s, 1]
        if outgoing:
            tall[0] = nn(grad, right)
            tall[1] = tn(grad, left)
        else:
            tall[0] = nt(right, grad)
            tall[1] = nn(left, grad)
        disperse(k_out)
        start(k_out)

    def unproject(s, w_in_ref, k, keep):
        await_all(k, rsem)
        unpack(k)
        for x in range(CHUNKS):
            left_grad, right_grad = take_pair(x)
            mask = mask_ref[0:1, at(x)]
            p = proj_ref[s, :, at(x)]
            dres = res_ref[s, :, at(x)]
            for side, grad in ((0, left_grad * mask), (2, right_grad * mask)):
                value = p[side * H : (side + 1) * H]
                sig = jax.nn.sigmoid(p[(side + 1) * H : (side + 2) * H])
                scaled = grad * sig
                pgr_ref[side * H : (side + 1) * H, at(x)] = scaled.astype(BF16)
                pgr_ref[(side + 1) * H : (side + 2) * H, at(x)] = (
                    scaled * value * (1.0 - sig)
                ).astype(BF16)
            gate = gate_ref[s, :, at(x)]
            pgr_ref[4 * H :, at(x)] = (
                lifted_ref[s, :, at(x)] * dres * gate * (1.0 - gate)
            ).astype(BF16)
            dy = nn(w_in_ref[...], pgr_ref[:, at(x)])
            grad = norm_grad(dy, y_ref[s, :, at(x)], yinv_ref[s, :, at(x)])
            keep(x, (dres + grad).astype(BF16))

    def sum_weights(s, k):
        w_in_grad = nt(n_ref[s], pgr_ref[...])
        for x in range(5):
            wide[pl.ds(x, H, stride=8), :] = w_in_grad[:, at(x)]
        wide[pl.ds(5, H, stride=8), :] = nt(tn_ref[s], lg_ref[...])
        wide[pl.ds(6, H, stride=8), :] = jnp.zeros((H, 128), F32)
        wide[pl.ds(7, H, stride=8), :] = jnp.zeros((H, 128), F32)
        pack(k)
        start(k)

    def share_weights(k_in, k_out, s):
        await_all(k_in, rsem)
        total = jnp.sum(got[k_in].astype(F32), axis=0)
        share[s] = (total * (1.0 / TOKENS)).astype(BF16)
        start_share(k_out, s)

    def give_weights(k, in_ref, out_ref):
        await_all(k, rsem)
        unpack(k)
        for x in range(5):
            in_ref[:, at(x)] = wide[pl.ds(x, H, stride=8), :]
        out_ref[...] = wide[pl.ds(5, H, stride=8), :]

    def write_tokens(ref, x, values):
        turned = values.astype(F32).T.astype(BF16)
        for m, i in enumerate(token_rows(x)):
            ref[i] = turned[16 * m : 16 * (m + 1)]

    def read_tokens(ref, x):
        return jnp.concatenate([ref[i] for i in token_rows(x)], axis=0).astype(F32).T

    lane = lax.broadcasted_iota(jnp.int32, (TOKENS, 512), 1)
    token = lax.broadcasted_iota(jnp.int32, (TOKENS, 512), 0)
    own_row = row * ROWS + ((lane >> 4) & 3) * 8 + ((lane >> 6) & 1) * 4 + (lane >> 7)
    own_col = col * COLS + (lane & 15)
    flags = jnp.broadcast_to(flags_ref[...].astype(F32), (8, TOKENS)).astype(BF16)
    row_flags = nn(flags, jnp.where(token == own_row, 1.0, 0.0).astype(BF16))
    col_flags = nn(flags, jnp.where(token == own_col, 1.0, 0.0).astype(BF16))
    mask_ref[...] = row_flags * col_flags

    set_weights(wio_ref, woo_ref, 0)
    for x in range(CHUNKS):
        z_ref[0, :, at(x)] = read_tokens(pair_ref, x)

    pl.semaphore_wait(bar, N - 1)
    project(0, OUT_LR)
    set_weights(wii_ref, woi_ref, 1)
    for x in range(CHUNKS):
        res_ref[1, :, at(x)] = read_tokens(cot_ref, x)
    multiply(0, OUT_LR, OUT_TRI, True)

    def keep_mid(x, mid):
        z_ref[1, :, at(x)] = mid.astype(F32)

    lift(0, OUT_TRI, keep_mid)
    project(1, IN_LR)
    multiply(1, IN_LR, IN_TRI, False)

    def keep_updated(x, updated):
        n_done = updated
        sides_ref[:, at(x)] = n_done

    lift(1, IN_TRI, keep_updated)
    back(1, woi_ref, IN_BACK)
    for x in range(CHUNKS):
        write_tokens(upd_ref, x, sides_ref[:, at(x)])
    side_products(1, IN_BACK, IN_SIDES, False)

    def keep_mid_grad(x, grad):
        res_ref[0, :, at(x)] = grad.astype(F32)

    unproject(1, wii_ref, IN_SIDES, keep_mid_grad)
    sum_weights(1, IN_SUM)
    back(0, woo_ref, OUT_BACK)
    side_products(0, OUT_BACK, OUT_SIDES, True)
    share_weights(IN_SUM, IN_SHARE, 0)

    def keep_pair_grad(x, grad):
        sides_ref[:, at(x)] = grad

    unproject(0, wio_ref, OUT_SIDES, keep_pair_grad)
    sum_weights(0, OUT_SUM)
    for x in range(CHUNKS):
        write_tokens(pg_ref, x, sides_ref[:, at(x)])
    give_weights(IN_SHARE, gii_ref, goi_ref)
    share_weights(OUT_SUM, OUT_SHARE, 1)
    give_weights(OUT_SHARE, gio_ref, goo_ref)
    for k in range(EXCHANGES):
        await_all(k, ssem)


def local(pair, cotangent, token_mask, out_in_proj, out_out_proj, in_in_proj, in_out_proj):
    tile = jax.ShapeDtypeStruct((ROWS, COLS, H), BF16)
    wide_grad = jax.ShapeDtypeStruct((H, 5 * H), F32)
    small_grad = jax.ShapeDtypeStruct((H, H), F32)
    vmem = pl.BlockSpec(memory_space=pltpu.VMEM)
    return pl.pallas_call(
        kernel,
        name="triangle_step",
        out_shape=(tile, tile, wide_grad, small_grad, wide_grad, small_grad),
        in_specs=[vmem] * 7,
        out_specs=(vmem,) * 6,
        scratch_shapes=[
            pltpu.VMEM((EXCHANGES, N, 8, 128), BF16),
            pltpu.VMEM((EXCHANGES, N, 8, 128), BF16),
            pltpu.VMEM((2, 8, 128), BF16),
            pltpu.VMEM((N * 8, 128), F32),
            pltpu.VMEM((2, 2, TOKENS, TOKENS), BF16),
            pltpu.VMEM((2, TOKENS, TOKENS), F32),
            pltpu.VMEM((8, 512), F32),
            pltpu.VMEM((2, H, 512), F32),
            pltpu.VMEM((2, H, 512), F32),
            pltpu.VMEM((2, 1, 512), F32),
            pltpu.VMEM((2, H, 512), BF16),
            pltpu.VMEM((2, 5 * H, 512), F32),
            pltpu.VMEM((2, H, 512), F32),
            pltpu.VMEM((2, H, 512), F32),
            pltpu.VMEM((2, 1, 512), F32),
            pltpu.VMEM((2, H, 512), BF16),
            pltpu.VMEM((2, H, 512), F32),
            pltpu.VMEM((H, 512), BF16),
            pltpu.VMEM((2, H, 512), F32),
            pltpu.VMEM((H, 512), BF16),
            pltpu.VMEM((5 * H, 512), BF16),
            pltpu.VMEM((2, 5 * H, H), BF16),
            pltpu.VMEM((2, H, H), BF16),
            pltpu.SemaphoreType.DMA((EXCHANGES,)),
            pltpu.SemaphoreType.DMA((EXCHANGES,)),
        ],
        compiler_params=pltpu.CompilerParams(
            collective_id=0, has_side_effects=True, vmem_limit_bytes=48 * 1024 * 1024
        ),
    )(
        pair, cotangent, token_mask.reshape(1, TOKENS),
        out_in_proj, out_out_proj, in_in_proj, in_out_proj,
    )


def solution(mesh):
    return jax.shard_map(
        local,
        mesh=mesh,
        in_specs=(P("row", "col", None), P("row", "col", None), P(), P(), P(), P(), P()),
        out_specs=(P("row", "col", None), P("row", "col", None), P(), P(), P(), P()),
        check_vma=False,
    )
```

time: 566 us -> 121 us (0.21)
  waiting for transfers between devices: 254 us -> 0 us
  local copies, waits for them, and re-layouts: 130 us -> 9.84 us
  Pallas kernels: 0 us -> 111 us
  blocking collectives: 71.5 us -> 0 us
  matrix products: 47.2 us -> 0 us
  starting transfers between devices: 23.8 us -> 0 us
  other arithmetic: 23.6 us -> 0 us
  between operations: 14.2 us -> 0.66 us
    psum x1 -> x0, waiting for transfers between devices: 146 us -> none  [local(): lax.psum((out_in_part, out_out_part, in_in_part, in_out_part), ('row', 'c...]
    pallas_call x0 -> x1, Pallas kernels: none -> 111 us  [local(): pl.pallas_call(kernel, name='triangle_step', out_shape=(tile, tile, wide_...]
    all_gather x4 -> x0, waiting for transfers between devices: 83.4 us -> none  [cols_of(): lax.all_gather(shortened(tiles), 'col', axis=1, tiled=True)]
    all_to_all x3 -> x0, blocking collectives: 71.5 us -> none  [the longest x2 40 us: from_everyone(): return lax.all_to_all(copies, axis, split_axis=0, concat_axis=0, tiled=True)]
    all_gather x6 -> x0, local copies, waits for them, and re-layouts: 69.7 us -> none  [cols_of(): lax.all_gather(shortened(tiles), 'col', axis=1, tiled=True)]
    dot_general x18 -> x0, matrix products: 47.2 us -> none  [the longest x1 6 us: outgoing_sum(): jnp.einsum('ikh,jkh->ijh', left_panel, right_rows, preferred_element_type...]
    all_to_all x8 -> x0, local copies, waits for them, and re-layouts: 26.3 us -> none  [the longest x4 17.2 us: to_col_blocks(): return lax.all_to_all(panel, 'row', split_axis=1, concat_axis=0, tiled=True)]
    all_to_all x5 -> x0, waiting for transfers between devices: 24.5 us -> none  [the longest x2 24.5 us: to_col_blocks(): return lax.all_to_all(panel, 'row', split_axis=1, concat_axis=0, tiled=True)]
  transfers between devices with their start and end apart: 10 -> 0, of which waited for: 5 -> 0; matrix products, arithmetic and copies ran while one was open for 20% -> 0% of each run, Pallas kernels for 0% -> 0%
where the time goes in v2:
time: 121 us
  Pallas kernels  111 us (92%)
  local copies, waits for them, and re-layouts  9.84 us (8%)
    pallas_call x1, Pallas kernels, local(): pl.pallas_call(kernel, name='triangle_step', out_shape=(tile, tile, wide_...  111 us
    unnamed x20, local copies, waits for them, and re-layouts  9.84 us

profile of v2, /device:TPU:1, one launch (start us, length us, event | category | flops | bytes accessed | tf_op | source)
XLA Modules:
  0.0 121.1 jit_solution(4477319423622925876)
XLA Ops:
  0.6 0.0 copy-start.6
  0.6 0.7 copy-done.6
  1.3 0.0 copy-start
  1.3 0.9 copy-done
  2.2 0.0 copy-start.1
  2.2 0.9 copy-done.1
  3.1 0.0 copy-start.2
  3.1 0.9 copy-done.2
  4.1 0.0 copy-start.3
  4.1 0.9 copy-done.3
  5.0 0.0 copy-start.4
  5.0 0.8 copy-done.4
  5.7 0.0 copy-start.5
  5.7 0.8 copy-done.5
  6.5 110.6 %triangle_step.1 = (bf16[32,16,128]{2,1,0:T(8,128)(2,1)S(1)}, bf16[32,16,128]{2,1,0:T(8,128)(2,1)S(1)}, f32[128,640]{1,0:T(8,128)S(1)}, f32[128,128]{1,0:T(8,128...) custom-call(bf16[32,16,128]{2,1,0:T(8,128)(2,1)S(1)} %copy-done.2, bf16[32,16,128]{2,1,0:T(8,128)(2,1)S(1)} %copy-done.3, ...), custom_call_target="tpu_custom_call" | custom-call | tf_op jit(solution)/shard_map/triangle_step/pallas_call | solution.py:351
  117.1 0.7 copy.19
  117.7 0.7 copy.20
  118.4 0.7 copy.21
  119.1 0.6 copy.22
  119.7 0.7 copy.23
  120.4 0.6 copy.24
Async XLA Ops:
  0.6 0.7 copy-start.6
  1.3 0.9 copy-start
  2.2 0.9 copy-start.1
  3.1 0.9 copy-start.2
  4.1 0.9 copy-start.3
  5.0 0.8 copy-start.4
  5.7 0.8 copy-start.5

commit v3 on v2

--- a/solution.py
+++ b/solution.py
@@ -73,29 +73,47 @@
 
 
 def kernel(
-    pair_ref, cot_ref, flags_ref, wio_ref, woo_ref, wii_ref, woi_ref,
+    pair_in, cot_in, flags_in, wio_in, woo_in, wii_in, woi_in,
     upd_ref, pg_ref, gio_ref, goo_ref, gii_ref, goi_ref,
     send, got, share, wide, mats, tall, mask_ref,
     z_ref, y_ref, yinv_ref, n_ref, proj_ref, gate_ref, t_ref, tinv_ref, tn_ref, lifted_ref,
     sides_ref, res_ref, lg_ref, pgr_ref, wint_ref, woutt_ref,
-    ssem, rsem,
+    pair_ref, cot_ref, flags_ref, wio_ref, woo_ref, wii_ref, woi_ref,
+    ssem, rsem, isem,
 ):
+    loads = [
+        pltpu.make_async_copy(src, dst, isem.at[n])
+        for n, (src, dst) in enumerate((
+            (pair_in, pair_ref), (wio_in, wio_ref), (flags_in, flags_ref), (woo_in, woo_ref),
+            (cot_in, cot_ref), (wii_in, wii_ref), (woi_in, woi_ref),
+        ))
+    ]
+    for load in loads:
+        load.start()
+
     cols = lax.axis_size("col")
     row, col = lax.axis_index("row"), lax.axis_index("col")
     me = row * cols + col
 
+    place_y, place_z, core = row // 2, col // 4, lax.rem(col, 2)
+    place_x = lax.rem(col, 4) // 2 * 2 + lax.rem(row, 2)
+
     def peer(step):
-        other = lax.rem(me + step, N)
-        return other // cols, lax.rem(other, cols)
+        def turned(place, digit):
+            return (place + (digit ^ (digit >> 1) ^ 2)) & 3
+
+        z, x = turned(place_z, step >> 5), turned(place_x, (step >> 3) & 3)
+        y, c = turned(place_y, (step >> 1) & 3), core ^ (step & 1) ^ 1
+        return y * 2 + (x & 1), z * 4 + (x >> 1) * 2 + c
 
     bar = pltpu.get_barrier_semaphore()
 
-    @pl.loop(1, N)
+    @pl.loop(0, N - 1)
     def _(step):
         pl.semaphore_signal(bar, inc=1, device_id=peer(step), device_id_type=MESH)
 
     def start(k):
-        @pl.loop(1, N)
+        @pl.loop(0, N - 1)
         def _(step):
             a, b = peer(step)
             pltpu.make_async_remote_copy(
@@ -106,7 +124,7 @@
         got[k, me] = send[k, me]
 
     def start_share(k, s):
-        @pl.loop(1, N)
+        @pl.loop(0, N - 1)
         def _(step):
             pltpu.make_async_remote_copy(
                 src_ref=share.at[s], dst_ref=got.at[k, me], send_sem=ssem.at[k],
@@ -134,31 +152,31 @@
         return halves(wide[pl.ds(x, H, stride=8), :], wide[pl.ds(4 + x, H, stride=8), :])
 
     def assemble(k):
-        @pl.loop(0, 8)
-        def _(r):
+        for r in range(8):
             for hi in range(2):
                 v = interchange([got[k, r * 16 + hi * 8 + lo].astype(F32) for lo in range(8)])
                 for t in range(2):
                     for ih in range(4):
-                        rows = pl.ds(pl.multiple_of(r * 32 + ih * 8, 8), 8)
+                        rows = slice(r * 32 + ih * 8, r * 32 + ih * 8 + 8)
                         tall[t, rows, at(hi)] = v[t * 4 + ih]
 
     def disperse(k):
-        @pl.loop(0, 8)
-        def _(r):
+        for r in range(8):
             for hi in range(2):
                 v = interchange([
-                    tall[t, pl.ds(pl.multiple_of(r * 32 + ih * 8, 8), 8), at(hi)]
+                    tall[t, slice(r * 32 + ih * 8, r * 32 + ih * 8 + 8), at(hi)]
                     for t in range(2) for ih in range(4)
                 ])
                 for lo in range(8):
                     send[k, r * 16 + hi * 8 + lo] = v[lo].astype(BF16)
 
-    def set_weights(w_in_ref, w_out_ref, s):
+    def set_in(w_in_ref, s):
         wint_ref[s] = w_in_ref[...].astype(F32).T.astype(BF16)
+
+    def set_out(w_out_ref, s):
         woutt_ref[s] = w_out_ref[...].astype(F32).T.astype(BF16)
 
-    def project(s, k):
+    def project(s, k, ready=lambda: None):
         for x in range(CHUNKS):
             y, inv = norm(z_ref[s, :, at(x)])
             y_ref[s, :, at(x)] = y
@@ -172,6 +190,7 @@
             right = jax.nn.sigmoid(p[3 * H : 4 * H]) * p[2 * H : 3 * H] * mask
             put_pair(x, left, right)
         pack(k)
+        ready()
         start(k)
         gate_ref[s] = jax.nn.sigmoid(proj_ref[s, 4 * H :, :])
 
@@ -207,7 +226,7 @@
         for x in range(CHUNKS):
             dres = res_ref[s, :, at(x)]
             lift_grad = (gate_ref[s, :, at(x)] * dres).astype(BF16)
-            lg_ref[:, at(x)] = lift_grad
+            lg_ref[s, :, at(x)] = lift_grad
             dy = nn(w_out_ref[...], lift_grad)
             tri_grad = norm_grad(dy, t_ref[s, :, at(x)], tinv_ref[s, :, at(x)])
             put_pair(x, tri_grad, jnp.zeros_like(tri_grad))
@@ -256,7 +275,7 @@
         w_in_grad = nt(n_ref[s], pgr_ref[...])
         for x in range(5):
             wide[pl.ds(x, H, stride=8), :] = w_in_grad[:, at(x)]
-        wide[pl.ds(5, H, stride=8), :] = nt(tn_ref[s], lg_ref[...])
+        wide[pl.ds(5, H, stride=8), :] = nt(tn_ref[s], lg_ref[s])
         wide[pl.ds(6, H, stride=8), :] = jnp.zeros((H, 128), F32)
         wide[pl.ds(7, H, stride=8), :] = jnp.zeros((H, 128), F32)
         pack(k)
@@ -282,6 +301,9 @@
 
     def read_tokens(ref, x):
         return jnp.concatenate([ref[i] for i in token_rows(x)], axis=0).astype(F32).T
+
+    for load in loads[:3]:
+        load.wait()
 
     lane = lax.broadcasted_iota(jnp.int32, (TOKENS, 512), 1)
     token = lax.broadcasted_iota(jnp.int32, (TOKENS, 512), 0)
@@ -292,13 +314,16 @@
     col_flags = nn(flags, jnp.where(token == own_col, 1.0, 0.0).astype(BF16))
     mask_ref[...] = row_flags * col_flags
 
-    set_weights(wio_ref, woo_ref, 0)
+    set_in(wio_ref, 0)
     for x in range(CHUNKS):
         z_ref[0, :, at(x)] = read_tokens(pair_ref, x)
 
-    pl.semaphore_wait(bar, N - 1)
-    project(0, OUT_LR)
-    set_weights(wii_ref, woi_ref, 1)
+    project(0, OUT_LR, lambda: pl.semaphore_wait(bar, N - 1))
+    for load in loads[3:]:
+        load.wait()
+    set_out(woo_ref, 0)
+    set_in(wii_ref, 1)
+    set_out(woi_ref, 1)
     for x in range(CHUNKS):
         res_ref[1, :, at(x)] = read_tokens(cot_ref, x)
     multiply(0, OUT_LR, OUT_TRI, True)
@@ -311,8 +336,7 @@
     multiply(1, IN_LR, IN_TRI, False)
 
     def keep_updated(x, updated):
-        n_done = updated
-        sides_ref[:, at(x)] = n_done
+        sides_ref[:, at(x)] = updated
 
     lift(1, IN_TRI, keep_updated)
     back(1, woi_ref, IN_BACK)
@@ -324,8 +348,8 @@
         res_ref[0, :, at(x)] = grad.astype(F32)
 
     unproject(1, wii_ref, IN_SIDES, keep_mid_grad)
+    back(0, woo_ref, OUT_BACK)
     sum_weights(1, IN_SUM)
-    back(0, woo_ref, OUT_BACK)
     side_products(0, OUT_BACK, OUT_SIDES, True)
     share_weights(IN_SUM, IN_SHARE, 0)
 
@@ -343,16 +367,28 @@
         await_all(k, ssem)
 
 
+def deliver(*refs):
+    copies = [
+        pltpu.make_async_copy(refs[n], refs[6 + n], refs[12].at[n]) for n in (2, 4, 0, 1, 3, 5)
+    ]
+    for copy in copies:
+        copy.start()
+    for copy in copies:
+        copy.wait()
+
+
 def local(pair, cotangent, token_mask, out_in_proj, out_out_proj, in_in_proj, in_out_proj):
     tile = jax.ShapeDtypeStruct((ROWS, COLS, H), BF16)
     wide_grad = jax.ShapeDtypeStruct((H, 5 * H), F32)
     small_grad = jax.ShapeDtypeStruct((H, H), F32)
     vmem = pl.BlockSpec(memory_space=pltpu.VMEM)
-    return pl.pallas_call(
+    far = pl.BlockSpec(memory_space=pltpu.HBM)
+    shapes = (tile, tile, wide_grad, small_grad, wide_grad, small_grad)
+    results = pl.pallas_call(
         kernel,
         name="triangle_step",
-        out_shape=(tile, tile, wide_grad, small_grad, wide_grad, small_grad),
-        in_specs=[vmem] * 7,
+        out_shape=tuple(pltpu.VMEM(s.shape, s.dtype) for s in shapes),
+        in_specs=[far] * 7,
         out_specs=(vmem,) * 6,
         scratch_shapes=[
             pltpu.VMEM((EXCHANGES, N, 8, 128), BF16),
@@ -374,20 +410,40 @@
             pltpu.VMEM((2, H, 512), F32),
             pltpu.VMEM((H, 512), BF16),
             pltpu.VMEM((2, H, 512), F32),
-            pltpu.VMEM((H, 512), BF16),
+            pltpu.VMEM((2, H, 512), BF16),
             pltpu.VMEM((5 * H, 512), BF16),
             pltpu.VMEM((2, 5 * H, H), BF16),
             pltpu.VMEM((2, H, H), BF16),
+            pltpu.VMEM((ROWS, COLS, H), BF16),
+            pltpu.VMEM((ROWS, COLS, H), BF16),
+            pltpu.VMEM((1, TOKENS), jnp.int32),
+            pltpu.VMEM((H, 5 * H), BF16),
+            pltpu.VMEM((H, H), BF16),
+            pltpu.VMEM((H, 5 * H), BF16),
+            pltpu.VMEM((H, H), BF16),
             pltpu.SemaphoreType.DMA((EXCHANGES,)),
             pltpu.SemaphoreType.DMA((EXCHANGES,)),
+            pltpu.SemaphoreType.DMA((7,)),
         ],
         compiler_params=pltpu.CompilerParams(
-            collective_id=0, has_side_effects=True, vmem_limit_bytes=48 * 1024 * 1024
+            collective_id=0, has_side_effects=True, vmem_limit_bytes=40 * 1024 * 1024
         ),
-    )(
-        pair, cotangent, token_mask.reshape(1, TOKENS),
-        out_in_proj, out_out_proj, in_in_proj, in_out_proj,
-    )
+    )(*(
+        pltpu.with_memory_space_constraint(array, pltpu.HBM)
+        for array in (
+            pair, cotangent, token_mask.reshape(1, TOKENS),
+            out_in_proj, out_out_proj, in_in_proj, in_out_proj,
+        )
+    ))
+    results = [pltpu.with_memory_space_constraint(r, pltpu.VMEM) for r in results]
+    return pl.pallas_call(
+        deliver,
+        name="deliver",
+        out_shape=shapes,
+        in_specs=[vmem] * 6,
+        out_specs=(far,) * 6,
+        scratch_shapes=[pltpu.SemaphoreType.DMA((6,))],
+    )(*results)
 
 
 def solution(mesh):

time: 121 us -> 92 us (0.76)
  Pallas kernels: 111 us -> 91.2 us
  local copies, waits for them, and re-layouts: 9.84 us -> 0 us
    pallas_call x1 -> x2, Pallas kernels: 111 us -> 91.2 us  [the longest x1 90.2 us: local(): pl.pallas_call(kernel, name='triangle_step', out_shape=tuple((pltpu.VMEM(...]
    unnamed x20 -> x0, local copies, waits for them, and re-layouts: 9.84 us -> none
where the time goes in v3:
time: 92 us; the launch traced here: 91.9 us
  Pallas kernels  91.2 us (99%)
    pallas_call x1, Pallas kernels, local(): pl.pallas_call(kernel, name='triangle_step', out_shape=tuple((pltpu.VMEM(...  90.2 us

profile of v3, /device:TPU:1, one launch (start us, length us, event | category | flops | bytes accessed | tf_op | source)
XLA Modules:
  0.0 91.9 jit_solution(14509593831361769778)
XLA Ops:
  0.6 90.2 %triangle_step.1 = (bf16[32,16,128]{2,1,0:T(8,128)(2,1)S(1)}, bf16[32,16,128]{2,1,0:T(8,128)(2,1)S(1)}, f32[128,640]{1,0:T(8,128)S(1)}, f32[128,128]{1,0:T(8,128...) custom-call(bf16[32,16,128]{2,1,0:T(8,128)(2,1)} %pair_in.1, bf16[32,16,128]{2,1,0:T(8,128)(2,1)} %cot_in.1, ...), custom_call_target="tpu_custom_call" | custom-call | tf_op jit(solution)/shard_map/triangle_step/pallas_call | solution.py:387
  90.9 1.0 %deliver.1 = (bf16[32,16,128]{2,1,0:T(8,128)(2,1)}, bf16[32,16,128]{2,1,0:T(8,128)(2,1)}, f32[128,640]{1,0:T(8,128)}, f32[128,128]{1,0:T(8,128)}, f32[128,640]{1,0:T(8,128)}, /*index=5*/f32[128,128]{1,0:T(8,128)}) custom-call(bf16[32,16,128]{2,1,0:T(8,128)(2,1)S(1)} %get-tuple-element.12.refs_0_, bf16[32,16,128]{2,1,0:T(8,128)(2,1)S(1)} %get-tuple-element.13.refs_1_, ...), custom_call_target="tpu_custom_call" | custom-call | tf_op jit(solution)/shard_map/deliver/pallas_call | solution.py:439

commit v4 on v3

--- a/solution.py
+++ b/solution.py
@@ -14,8 +14,8 @@
 ROWS, COLS = 32, 16
 CHUNKS = 4
 TOKENS = 256
-OUT_LR, OUT_TRI, IN_LR, IN_TRI, IN_BACK, IN_SIDES, OUT_BACK, OUT_SIDES = range(8)
-IN_SUM, IN_SHARE, OUT_SUM, OUT_SHARE = range(8, 12)
+OUT_LR, IN_LR, IN_SIDES, OUT_SIDES, IN_SUM, IN_SHARE = range(6)
+OUT_TRI, IN_TRI, IN_BACK, OUT_BACK, OUT_SUM, OUT_SHARE = range(6, 12)
 EXCHANGES = 12
 
 
@@ -75,7 +75,7 @@
 def kernel(
     pair_in, cot_in, flags_in, wio_in, woo_in, wii_in, woi_in,
     upd_ref, pg_ref, gio_ref, goo_ref, gii_ref, goi_ref,
-    send, got, share, wide, mats, tall, mask_ref,
+    send8, got8, send4, got4, share8, share4, wide, mats, tall, mask_ref,
     z_ref, y_ref, yinv_ref, n_ref, proj_ref, gate_ref, t_ref, tinv_ref, tn_ref, lifted_ref,
     sides_ref, res_ref, lg_ref, pgr_ref, wint_ref, woutt_ref,
     pair_ref, cot_ref, flags_ref, wio_ref, woo_ref, wii_ref, woi_ref,
@@ -112,29 +112,39 @@
     def _(step):
         pl.semaphore_signal(bar, inc=1, device_id=peer(step), device_id_type=MESH)
 
+    def sent(k):
+        return send8.at[k] if k < 6 else send4.at[k - 6]
+
+    def got(k):
+        return got8.at[k] if k < 6 else got4.at[k - 6]
+
     def start(k):
+        source, target = sent(k), got(k)
+
         @pl.loop(0, N - 1)
         def _(step):
             a, b = peer(step)
             pltpu.make_async_remote_copy(
-                src_ref=send.at[k, a * cols + b], dst_ref=got.at[k, me], send_sem=ssem.at[k],
+                src_ref=source.at[a * cols + b], dst_ref=target.at[me], send_sem=ssem.at[k],
                 recv_sem=rsem.at[k], device_id=(a, b), device_id_type=MESH,
             ).start()
 
-        got[k, me] = send[k, me]
-
-    def start_share(k, s):
+        target[me] = source[me]
+
+    def start_share(k):
+        source, target = share8 if k < 6 else share4, got(k)
+
         @pl.loop(0, N - 1)
         def _(step):
             pltpu.make_async_remote_copy(
-                src_ref=share.at[s], dst_ref=got.at[k, me], send_sem=ssem.at[k],
+                src_ref=source, dst_ref=target.at[me], send_sem=ssem.at[k],
                 recv_sem=rsem.at[k], device_id=peer(step), device_id_type=MESH,
             ).start()
 
-        got[k, me] = share[s]
+        target[me] = source[...]
 
     def await_all(k, sem):
-        part = got.at[k, pl.ds(0, N - 1)]
+        part = got(k).at[pl.ds(0, N - 1)]
         pltpu.make_async_copy(part, part, sem.at[k]).wait()
 
     def put_pair(x, left, right):
@@ -142,33 +152,55 @@
         wide[pl.ds(x, H, stride=8), :] = first
         wide[pl.ds(4 + x, H, stride=8), :] = second
 
+    def put(x, value):
+        wide[pl.ds(x, H, stride=4), :] = value
+
     def pack(k):
-        send[k] = wide[...].reshape(N, 8, 128).astype(BF16)
+        if k < 6:
+            sent(k)[...] = wide[...].reshape(N, 8, 128).astype(BF16)
+            return
+        for pair in range(N // 2):
+            both = wide[8 * pair : 8 * pair + 8, :]
+            sent(k)[2 * pair] = both[:4].astype(BF16)
+            sent(k)[2 * pair + 1] = both[4:].astype(BF16)
 
     def unpack(k):
-        wide[...] = got[k].astype(F32).reshape(N * 8, 128)
+        if k < 6:
+            wide[...] = got(k)[...].astype(F32).reshape(N * 8, 128)
+            return
+        for n in range(N):
+            wide[4 * n : 4 * n + 4, :] = got(k)[n].astype(F32)
 
     def take_pair(x):
         return halves(wide[pl.ds(x, H, stride=8), :], wide[pl.ds(4 + x, H, stride=8), :])
+
+    def take(x):
+        return wide[pl.ds(x, H, stride=4), :]
+
+    def spots(k, r, hi):
+        if k < 6:
+            return [
+                (t, slice(r * 32 + ih * 8, r * 32 + ih * 8 + 8), at(hi))
+                for t in range(2) for ih in range(4)
+            ]
+        return [
+            (0, slice(r * 32 + ih * 8 + b * 4, r * 32 + ih * 8 + b * 4 + 4), at(hi))
+            for b in range(2) for ih in range(4)
+        ]
 
     def assemble(k):
         for r in range(8):
             for hi in range(2):
-                v = interchange([got[k, r * 16 + hi * 8 + lo].astype(F32) for lo in range(8)])
-                for t in range(2):
-                    for ih in range(4):
-                        rows = slice(r * 32 + ih * 8, r * 32 + ih * 8 + 8)
-                        tall[t, rows, at(hi)] = v[t * 4 + ih]
+                v = interchange([got(k)[r * 16 + hi * 8 + lo].astype(F32) for lo in range(8)])
+                for spot, part in zip(spots(k, r, hi), v):
+                    tall[spot] = part
 
     def disperse(k):
         for r in range(8):
             for hi in range(2):
-                v = interchange([
-                    tall[t, slice(r * 32 + ih * 8, r * 32 + ih * 8 + 8), at(hi)]
-                    for t in range(2) for ih in range(4)
-                ])
+                v = interchange([tall[spot] for spot in spots(k, r, hi)])
                 for lo in range(8):
-                    send[k, r * 16 + hi * 8 + lo] = v[lo].astype(BF16)
+                    sent(k)[r * 16 + hi * 8 + lo] = v[lo].astype(BF16)
 
     def set_in(w_in_ref, s):
         wint_ref[s] = w_in_ref[...].astype(F32).T.astype(BF16)
@@ -199,12 +231,9 @@
         assemble(k_in)
         mats[s] = tall[...].astype(BF16)
         if outgoing:
-            tri = nt(mats[s, 0], mats[s, 1])
+            tall[0] = nt(mats[s, 0], mats[s, 1])
         else:
-            tri = tn(mats[s, 0], mats[s, 1])
-        high = tri.astype(BF16).astype(F32)
-        tall[0] = high
-        tall[1] = tri - high
+            tall[0] = tn(mats[s, 0], mats[s, 1])
         disperse(k_out)
         start(k_out)
 
@@ -212,8 +241,7 @@
         await_all(k, rsem)
         unpack(k)
         for x in range(CHUNKS):
-            high, low = take_pair(x)
-            y, inv = norm(high + low)
+            y, inv = norm(take(x))
             t_ref[s, :, at(x)] = y
             tinv_ref[s, :, at(x)] = inv
             normed = y.astype(BF16)
@@ -229,9 +257,14 @@
             lg_ref[s, :, at(x)] = lift_grad
             dy = nn(w_out_ref[...], lift_grad)
             tri_grad = norm_grad(dy, t_ref[s, :, at(x)], tinv_ref[s, :, at(x)])
-            put_pair(x, tri_grad, jnp.zeros_like(tri_grad))
+            put(x, tri_grad)
         pack(k)
         start(k)
+        for x in range(CHUNKS):
+            gate = gate_ref[s, :, at(x)]
+            pgr_ref[s, 4 * H :, at(x)] = (
+                lifted_ref[s, :, at(x)] * res_ref[s, :, at(x)] * gate * (1.0 - gate)
+            ).astype(BF16)
 
     def side_products(s, k_in, k_out, outgoing):
         await_all(k_in, rsem)
@@ -259,40 +292,54 @@
                 value = p[side * H : (side + 1) * H]
                 sig = jax.nn.sigmoid(p[(side + 1) * H : (side + 2) * H])
                 scaled = grad * sig
-                pgr_ref[side * H : (side + 1) * H, at(x)] = scaled.astype(BF16)
-                pgr_ref[(side + 1) * H : (side + 2) * H, at(x)] = (
+                pgr_ref[s, side * H : (side + 1) * H, at(x)] = scaled.astype(BF16)
+                pgr_ref[s, (side + 1) * H : (side + 2) * H, at(x)] = (
                     scaled * value * (1.0 - sig)
                 ).astype(BF16)
-            gate = gate_ref[s, :, at(x)]
-            pgr_ref[4 * H :, at(x)] = (
-                lifted_ref[s, :, at(x)] * dres * gate * (1.0 - gate)
-            ).astype(BF16)
-            dy = nn(w_in_ref[...], pgr_ref[:, at(x)])
+            dy = nn(w_in_ref[...], pgr_ref[s, :, at(x)])
             grad = norm_grad(dy, y_ref[s, :, at(x)], yinv_ref[s, :, at(x)])
             keep(x, (dres + grad).astype(BF16))
 
-    def sum_weights(s, k):
-        w_in_grad = nt(n_ref[s], pgr_ref[...])
+    def sum_early():
+        w_in_grad = nt(n_ref[1], pgr_ref[1])
         for x in range(5):
             wide[pl.ds(x, H, stride=8), :] = w_in_grad[:, at(x)]
-        wide[pl.ds(5, H, stride=8), :] = nt(tn_ref[s], lg_ref[s])
-        wide[pl.ds(6, H, stride=8), :] = jnp.zeros((H, 128), F32)
-        wide[pl.ds(7, H, stride=8), :] = jnp.zeros((H, 128), F32)
-        pack(k)
-        start(k)
-
-    def share_weights(k_in, k_out, s):
+        wide[pl.ds(5, H, stride=8), :] = nt(tn_ref[1], lg_ref[1])
+        wide[pl.ds(6, H, stride=8), :] = nt(tn_ref[0], lg_ref[0])
+        wide[pl.ds(7, H, stride=8), :] = nt(n_ref[0], pgr_ref[0, 4 * H :, :])
+        pack(IN_SUM)
+        start(IN_SUM)
+
+    def sum_late():
+        w_in_grad = nt(n_ref[0], pgr_ref[0, : 4 * H, :])
+        for x in range(4):
+            put(x, w_in_grad[:, at(x)])
+        pack(OUT_SUM)
+        start(OUT_SUM)
+
+    def share_sums(k_in, k_out):
         await_all(k_in, rsem)
-        total = jnp.sum(got[k_in].astype(F32), axis=0)
-        share[s] = (total * (1.0 / TOKENS)).astype(BF16)
-        start_share(k_out, s)
-
-    def give_weights(k, in_ref, out_ref):
-        await_all(k, rsem)
-        unpack(k)
+        total = jnp.sum(got(k_in)[...].astype(F32), axis=0) * (1.0 / TOKENS)
+        if k_in < 6:
+            share8[...] = total.astype(BF16)
+        else:
+            share4[...] = total.astype(BF16)
+        start_share(k_out)
+
+    def give_early():
+        await_all(IN_SHARE, rsem)
+        unpack(IN_SHARE)
         for x in range(5):
-            in_ref[:, at(x)] = wide[pl.ds(x, H, stride=8), :]
-        out_ref[...] = wide[pl.ds(5, H, stride=8), :]
+            gii_ref[:, at(x)] = wide[pl.ds(x, H, stride=8), :]
+        goi_ref[...] = wide[pl.ds(5, H, stride=8), :]
+        goo_ref[...] = wide[pl.ds(6, H, stride=8), :]
+        gio_ref[:, at(4)] = wide[pl.ds(7, H, stride=8), :]
+
+    def give_late():
+        await_all(OUT_SHARE, rsem)
+        unpack(OUT_SHARE)
+        for x in range(4):
+            gio_ref[:, at(x)] = take(x)
 
     def write_tokens(ref, x, values):
         turned = values.astype(F32).T.astype(BF16)
@@ -349,20 +396,20 @@
 
     unproject(1, wii_ref, IN_SIDES, keep_mid_grad)
     back(0, woo_ref, OUT_BACK)
-    sum_weights(1, IN_SUM)
+    sum_early()
     side_products(0, OUT_BACK, OUT_SIDES, True)
-    share_weights(IN_SUM, IN_SHARE, 0)
+    share_sums(IN_SUM, IN_SHARE)
 
     def keep_pair_grad(x, grad):
         sides_ref[:, at(x)] = grad
 
     unproject(0, wio_ref, OUT_SIDES, keep_pair_grad)
-    sum_weights(0, OUT_SUM)
+    sum_late()
     for x in range(CHUNKS):
         write_tokens(pg_ref, x, sides_ref[:, at(x)])
-    give_weights(IN_SHARE, gii_ref, goi_ref)
-    share_weights(OUT_SUM, OUT_SHARE, 1)
-    give_weights(OUT_SHARE, gio_ref, goo_ref)
+    give_early()
+    share_sums(OUT_SUM, OUT_SHARE)
+    give_late()
     for k in range(EXCHANGES):
         await_all(k, ssem)
 
@@ -391,9 +438,12 @@
         in_specs=[far] * 7,
         out_specs=(vmem,) * 6,
         scratch_shapes=[
-            pltpu.VMEM((EXCHANGES, N, 8, 128), BF16),
-            pltpu.VMEM((EXCHANGES, N, 8, 128), BF16),
-            pltpu.VMEM((2, 8, 128), BF16),
+            pltpu.VMEM((6, N, 8, 128), BF16),
+            pltpu.VMEM((6, N, 8, 128), BF16),
+            pltpu.VMEM((6, N, 4, 128), BF16),
+            pltpu.VMEM((6, N, 4, 128), BF16),
+            pltpu.VMEM((8, 128), BF16),
+            pltpu.VMEM((4, 128), BF16),
             pltpu.VMEM((N * 8, 128), F32),
             pltpu.VMEM((2, 2, TOKENS, TOKENS), BF16),
             pltpu.VMEM((2, TOKENS, TOKENS), F32),
@@ -411,7 +461,7 @@
             pltpu.VMEM((H, 512), BF16),
             pltpu.VMEM((2, H, 512), F32),
             pltpu.VMEM((2, H, 512), BF16),
-            pltpu.VMEM((5 * H, 512), BF16),
+            pltpu.VMEM((2, 5 * H, 512), BF16),
             pltpu.VMEM((2, 5 * H, H), BF16),
             pltpu.VMEM((2, H, H), BF16),
             pltpu.VMEM((ROWS, COLS, H), BF16),

time: 92 us -> 89.9 us (0.977)
  Pallas kernels: 91.2 us -> 89.2 us
    pallas_call x1, Pallas kernels: 90.2 us -> 88.2 us  [local(): pl.pallas_call(kernel, name='triangle_step', out_shape=tuple((pltpu.VMEM(...]
where the time goes in v4:
time: 89.9 us; the launch traced here: 89.8 us
  Pallas kernels  89.2 us (99%)
    pallas_call x1, Pallas kernels, local(): pl.pallas_call(kernel, name='triangle_step', out_shape=tuple((pltpu.VMEM(...  88.2 us

profile of v4, /device:TPU:1, one launch (start us, length us, event | category | flops | bytes accessed | tf_op | source)
XLA Modules:
  0.0 89.8 jit_solution(17484006020810059398)
XLA Ops:
  0.6 88.2 %triangle_step.1 = (bf16[32,16,128]{2,1,0:T(8,128)(2,1)S(1)}, bf16[32,16,128]{2,1,0:T(8,128)(2,1)S(1)}, f32[128,640]{1,0:T(8,128)S(1)}, f32[128,128]{1,0:T(8,128...) custom-call(bf16[32,16,128]{2,1,0:T(8,128)(2,1)} %pair_in.1, bf16[32,16,128]{2,1,0:T(8,128)(2,1)} %cot_in.1, ...), custom_call_target="tpu_custom_call" | custom-call | tf_op jit(solution)/shard_map/triangle_step/pallas_call | solution.py:434
  88.8 1.0 %deliver.1 = (bf16[32,16,128]{2,1,0:T(8,128)(2,1)}, bf16[32,16,128]{2,1,0:T(8,128)(2,1)}, f32[128,640]{1,0:T(8,128)}, f32[128,128]{1,0:T(8,128)}, f32[128,640]{1,0:T(8,128)}, /*index=5*/f32[128,128]{1,0:T(8,128)}) custom-call(bf16[32,16,128]{2,1,0:T(8,128)(2,1)S(1)} %get-tuple-element.12.refs_0_, bf16[32,16,128]{2,1,0:T(8,128)(2,1)S(1)} %get-tuple-element.13.refs_1_, ...), custom_call_target="tpu_custom_call" | custom-call | tf_op jit(solution)/shard_map/deliver/pallas_call | solution.py:489

commit v5 on v4

--- a/solution.py
+++ b/solution.py
@@ -53,23 +53,18 @@
 
 def halves(a, b):
     low = lax.broadcasted_iota(jnp.int32, a.shape, 1) < 64
-    return jnp.where(low, a, pltpu.roll(b, 64, 1)), jnp.where(low, pltpu.roll(a, 64, 1), b)
+    moved = pltpu.roll(jnp.where(low, b, a), 64, 1)
+    return jnp.where(low, a, moved), jnp.where(low, moved, b)
 
 
 def interchange(v):
-    v = list(v)
-    lane = lax.broadcasted_iota(jnp.int32, v[0].shape, 1)
-    for bit in range(3):
-        step = 16 << bit
-        low = (lane & step) == 0
-        for u in range(8):
-            w = u | (1 << bit)
-            if w == u:
-                continue
-            a, b = v[u], v[w]
-            v[u] = jnp.where(low, a, pltpu.roll(b, step, 1))
-            v[w] = jnp.where(low, pltpu.roll(a, 128 - step, 1), b)
-    return v
+    group = lax.broadcasted_iota(jnp.int32, v[0].shape, 1) >> 4
+    v = [v[0]] + [pltpu.roll(v[i], 16 * i, 1) for i in range(1, 8)]
+    v = [v[-j % 8] for j in range(8)]
+    for bit in (1, 2, 4):
+        here = (group & bit) != 0
+        v = [jnp.where(here, v[(j - bit) % 8], v[j]) for j in range(8)]
+    return [v[0]] + [pltpu.roll(v[j], 128 - 16 * j, 1) for j in range(1, 8)]
 
 
 def kernel(
@@ -98,19 +93,30 @@
     place_y, place_z, core = row // 2, col // 4, lax.rem(col, 2)
     place_x = lax.rem(col, 4) // 2 * 2 + lax.rem(row, 2)
 
-    def peer(step):
-        def turned(place, digit):
-            return (place + (digit ^ (digit >> 1) ^ 2)) & 3
-
-        z, x = turned(place_z, step >> 5), turned(place_x, (step >> 3) & 3)
-        y, c = turned(place_y, (step >> 1) & 3), core ^ (step & 1) ^ 1
-        return y * 2 + (x & 1), z * 4 + (x >> 1) * 2 + c
+    def turned(place, digit):
+        return (place + (digit ^ (digit >> 1) ^ 2)) & 3
+
+    others = [
+        (turned(place_y, digit) * 2, core ^ last ^ 1) for digit in range(4) for last in range(2)
+    ]
+
+    def to_others(send):
+        def some(step, among):
+            z, x = turned(place_z, step >> 2), turned(place_x, step & 3)
+            for y, c in among:
+                send(y + (x & 1), z * 4 + (x >> 1) * 2 + c)
+
+        @pl.loop(0, 15)
+        def _(step):
+            some(step, others)
+
+        some(15, others[:-1])
 
     bar = pltpu.get_barrier_semaphore()
 
-    @pl.loop(0, N - 1)
-    def _(step):
-        pl.semaphore_signal(bar, inc=1, device_id=peer(step), device_id_type=MESH)
+    to_others(
+        lambda a, b: pl.semaphore_signal(bar, inc=1, device_id=(a, b), device_id_type=MESH)
+    )
 
     def sent(k):
         return send8.at[k] if k < 6 else send4.at[k - 6]
@@ -121,26 +127,19 @@
     def start(k):
         source, target = sent(k), got(k)
 
-        @pl.loop(0, N - 1)
-        def _(step):
-            a, b = peer(step)
-            pltpu.make_async_remote_copy(
-                src_ref=source.at[a * cols + b], dst_ref=target.at[me], send_sem=ssem.at[k],
-                recv_sem=rsem.at[k], device_id=(a, b), device_id_type=MESH,
-            ).start()
-
+        to_others(lambda a, b: pltpu.make_async_remote_copy(
+            src_ref=source.at[a * cols + b], dst_ref=target.at[me], send_sem=ssem.at[k],
+            recv_sem=rsem.at[k], device_id=(a, b), device_id_type=MESH,
+        ).start())
         target[me] = source[me]
 
     def start_share(k):
         source, target = share8 if k < 6 else share4, got(k)
 
-        @pl.loop(0, N - 1)
-        def _(step):
-            pltpu.make_async_remote_copy(
-                src_ref=source, dst_ref=target.at[me], send_sem=ssem.at[k],
-                recv_sem=rsem.at[k], device_id=peer(step), device_id_type=MESH,
-            ).start()
-
+        to_others(lambda a, b: pltpu.make_async_remote_copy(
+            src_ref=source, dst_ref=target.at[me], send_sem=ssem.at[k],
+            recv_sem=rsem.at[k], device_id=(a, b), device_id_type=MESH,
+        ).start())
         target[me] = source[...]
 
     def await_all(k, sem):
@@ -280,14 +279,13 @@
         disperse(k_out)
         start(k_out)
 
-    def unproject(s, w_in_ref, k, keep):
+    def side_grads(s, k):
         await_all(k, rsem)
         unpack(k)
         for x in range(CHUNKS):
             left_grad, right_grad = take_pair(x)
             mask = mask_ref[0:1, at(x)]
             p = proj_ref[s, :, at(x)]
-            dres = res_ref[s, :, at(x)]
             for side, grad in ((0, left_grad * mask), (2, right_grad * mask)):
                 value = p[side * H : (side + 1) * H]
                 sig = jax.nn.sigmoid(p[(side + 1) * H : (side + 2) * H])
@@ -296,6 +294,10 @@
                 pgr_ref[s, (side + 1) * H : (side + 2) * H, at(x)] = (
                     scaled * value * (1.0 - sig)
                 ).astype(BF16)
+
+    def unproject(s, w_in_ref, keep):
+        for x in range(CHUNKS):
+            dres = res_ref[s, :, at(x)]
             dy = nn(w_in_ref[...], pgr_ref[s, :, at(x)])
             grad = norm_grad(dy, y_ref[s, :, at(x)], yinv_ref[s, :, at(x)])
             keep(x, (dres + grad).astype(BF16))
@@ -394,7 +396,8 @@
     def keep_mid_grad(x, grad):
         res_ref[0, :, at(x)] = grad.astype(F32)
 
-    unproject(1, wii_ref, IN_SIDES, keep_mid_grad)
+    side_grads(1, IN_SIDES)
+    unproject(1, wii_ref, keep_mid_grad)
     back(0, woo_ref, OUT_BACK)
     sum_early()
     side_products(0, OUT_BACK, OUT_SIDES, True)
@@ -403,8 +406,9 @@
     def keep_pair_grad(x, grad):
         sides_ref[:, at(x)] = grad
 
-    unproject(0, wio_ref, OUT_SIDES, keep_pair_grad)
+    side_grads(0, OUT_SIDES)
     sum_late()
+    unproject(0, wio_ref, keep_pair_grad)
     for x in range(CHUNKS):
         write_tokens(pg_ref, x, sides_ref[:, at(x)])
     give_early()

time: 89.9 us -> 88.2 us (0.981)
  Pallas kernels: 89.2 us -> 87.4 us
    pallas_call x1, Pallas kernels: 88.2 us -> 86.4 us  [local(): pl.pallas_call(kernel, name='triangle_step', out_shape=tuple((pltpu.VMEM(...]
where the time goes in v5:
time: 88.2 us; the launch traced here: 88.1 us
  Pallas kernels  87.4 us (99%)
    pallas_call x1, Pallas kernels, local(): pl.pallas_call(kernel, name='triangle_step', out_shape=tuple((pltpu.VMEM(...  86.4 us

profile of v5, /device:TPU:1, one launch (start us, length us, event | category | flops | bytes accessed | tf_op | source)
XLA Modules:
  0.0 88.1 jit_solution(18210911694051200272)
XLA Ops:
  0.6 86.4 %triangle_step.1 = (bf16[32,16,128]{2,1,0:T(8,128)(2,1)S(1)}, bf16[32,16,128]{2,1,0:T(8,128)(2,1)S(1)}, f32[128,640]{1,0:T(8,128)S(1)}, f32[128,128]{1,0:T(8,128...) custom-call(bf16[32,16,128]{2,1,0:T(8,128)(2,1)} %pair_in.1, bf16[32,16,128]{2,1,0:T(8,128)(2,1)} %cot_in.1, ...), custom_call_target="tpu_custom_call" | custom-call | tf_op jit(solution)/shard_map/triangle_step/pallas_call | solution.py:438
  87.1 1.0 %deliver.1 = (bf16[32,16,128]{2,1,0:T(8,128)(2,1)}, bf16[32,16,128]{2,1,0:T(8,128)(2,1)}, f32[128,640]{1,0:T(8,128)}, f32[128,128]{1,0:T(8,128)}, f32[128,640]{1,0:T(8,128)}, /*index=5*/f32[128,128]{1,0:T(8,128)}) custom-call(bf16[32,16,128]{2,1,0:T(8,128)(2,1)S(1)} %get-tuple-element.12.refs_0_, bf16[32,16,128]{2,1,0:T(8,128)(2,1)S(1)} %get-tuple-element.13.refs_1_, ...), custom_call_target="tpu_custom_call" | custom-call | tf_op jit(solution)/shard_map/deliver/pallas_call | solution.py:493

commit v6 on v5

--- a/solution.py
+++ b/solution.py
@@ -94,23 +94,26 @@
     place_x = lax.rem(col, 4) // 2 * 2 + lax.rem(row, 2)
 
     def turned(place, digit):
-        return (place + (digit ^ (digit >> 1) ^ 2)) & 3
+        return (place + (digit ^ (digit >> 1) ^ 2) * (1 - 2 * core)) & 3
 
     others = [
         (turned(place_y, digit) * 2, core ^ last ^ 1) for digit in range(4) for last in range(2)
     ]
 
     def to_others(send):
-        def some(step, among):
-            z, x = turned(place_z, step >> 2), turned(place_x, step & 3)
+        def some(z, x, among):
             for y, c in among:
                 send(y + (x & 1), z * 4 + (x >> 1) * 2 + c)
 
-        @pl.loop(0, 15)
+        xs = [turned(place_x, digit) for digit in range(4)]
+
+        @pl.loop(0, 3)
         def _(step):
-            some(step, others)
-
-        some(15, others[:-1])
+            for x in xs:
+                some(turned(place_z, step), x, others)
+
+        for n, x in enumerate(xs):
+            some(place_z, x, others if n < 3 else others[:-1])
 
     bar = pltpu.get_barrier_semaphore()
 
@@ -321,7 +324,12 @@
 
     def share_sums(k_in, k_out):
         await_all(k_in, rsem)
-        total = jnp.sum(got(k_in)[...].astype(F32), axis=0) * (1.0 / TOKENS)
+        parts = [
+            jnp.sum(got(k_in)[n : n + 16].astype(F32), axis=0) for n in range(0, N, 16)
+        ]
+        while len(parts) > 1:
+            parts = [a + b for a, b in zip(parts[::2], parts[1::2])]
+        total = parts[0] * (1.0 / TOKENS)
         if k_in < 6:
             share8[...] = total.astype(BF16)
         else:

time: 88.2 us -> 87.6 us (level)
  no operation moved by 1% of the time
where the time goes in v6:
time: 87.6 us; the launch traced here: 87.4 us
  Pallas kernels  86.8 us (99%)
    pallas_call x1, Pallas kernels, local(): pl.pallas_call(kernel, name='triangle_step', out_shape=tuple((pltpu.VMEM(...  85.8 us

profile of v6, /device:TPU:1, one launch (start us, length us, event | category | flops | bytes accessed | tf_op | source)
XLA Modules:
  0.0 87.4 jit_solution(9869522439009788505)
XLA Ops:
  0.6 85.8 %triangle_step.1 = (bf16[32,16,128]{2,1,0:T(8,128)(2,1)S(1)}, bf16[32,16,128]{2,1,0:T(8,128)(2,1)S(1)}, f32[128,640]{1,0:T(8,128)S(1)}, f32[128,128]{1,0:T(8,128...) custom-call(bf16[32,16,128]{2,1,0:T(8,128)(2,1)} %pair_in.1, bf16[32,16,128]{2,1,0:T(8,128)(2,1)} %cot_in.1, ...), custom_call_target="tpu_custom_call" | custom-call | tf_op jit(solution)/shard_map/triangle_step/pallas_call | solution.py:446
  86.4 1.0 %deliver.1 = (bf16[32,16,128]{2,1,0:T(8,128)(2,1)}, bf16[32,16,128]{2,1,0:T(8,128)(2,1)}, f32[128,640]{1,0:T(8,128)}, f32[128,128]{1,0:T(8,128)}, f32[128,640]{1,0:T(8,128)}, /*index=5*/f32[128,128]{1,0:T(8,128)}) custom-call(bf16[32,16,128]{2,1,0:T(8,128)(2,1)S(1)} %get-tuple-element.12.refs_0_, bf16[32,16,128]{2,1,0:T(8,128)(2,1)S(1)} %get-tuple-element.13.refs_1_, ...), custom_call_target="tpu_custom_call" | custom-call | tf_op jit(solution)/shard_map/deliver/pallas_call | solution.py:501

commit v7 on v6

--- a/solution.py
+++ b/solution.py
@@ -220,8 +220,11 @@
             mask = mask_ref[0:1, at(x)]
             p = nn(wint_ref[s], normed)
             proj_ref[s, :, at(x)] = p
-            left = jax.nn.sigmoid(p[H : 2 * H]) * p[:H] * mask
-            right = jax.nn.sigmoid(p[3 * H : 4 * H]) * p[2 * H : 3 * H] * mask
+            left_sig, right_sig = jax.nn.sigmoid(p[H : 2 * H]), jax.nn.sigmoid(p[3 * H : 4 * H])
+            proj_ref[s, H : 2 * H, at(x)] = left_sig
+            proj_ref[s, 3 * H : 4 * H, at(x)] = right_sig
+            left = left_sig * p[:H] * mask
+            right = right_sig * p[2 * H : 3 * H] * mask
             put_pair(x, left, right)
         pack(k)
         ready()
@@ -291,7 +294,7 @@
             p = proj_ref[s, :, at(x)]
             for side, grad in ((0, left_grad * mask), (2, right_grad * mask)):
                 value = p[side * H : (side + 1) * H]
-                sig = jax.nn.sigmoid(p[(side + 1) * H : (side + 2) * H])
+                sig = p[(side + 1) * H : (side + 2) * H]
                 scaled = grad * sig
                 pgr_ref[s, side * H : (side + 1) * H, at(x)] = scaled.astype(BF16)
                 pgr_ref[s, (side + 1) * H : (side + 2) * H, at(x)] = (

time: 87.6 us -> 87.5 us (level)
  no operation moved by 1% of the time
where the time goes in v7:
time: 87.5 us; the launch traced here: 87.4 us
  Pallas kernels  86.8 us (99%)
    pallas_call x1, Pallas kernels, local(): pl.pallas_call(kernel, name='triangle_step', out_shape=tuple((pltpu.VMEM(...  85.8 us

profile of v7, /device:TPU:1, one launch (start us, length us, event | category | flops | bytes accessed | tf_op | source)
XLA Modules:
  0.0 87.4 jit_solution(9604090532485978279)
XLA Ops:
  0.6 85.8 %triangle_step.1 = (bf16[32,16,128]{2,1,0:T(8,128)(2,1)S(1)}, bf16[32,16,128]{2,1,0:T(8,128)(2,1)S(1)}, f32[128,640]{1,0:T(8,128)S(1)}, f32[128,128]{1,0:T(8,128...) custom-call(bf16[32,16,128]{2,1,0:T(8,128)(2,1)} %pair_in.1, bf16[32,16,128]{2,1,0:T(8,128)(2,1)} %cot_in.1, ...), custom_call_target="tpu_custom_call" | custom-call | tf_op jit(solution)/shard_map/triangle_step/pallas_call | solution.py:449
  86.4 1.0 %deliver.1 = (bf16[32,16,128]{2,1,0:T(8,128)(2,1)}, bf16[32,16,128]{2,1,0:T(8,128)(2,1)}, f32[128,640]{1,0:T(8,128)}, f32[128,128]{1,0:T(8,128)}, f32[128,640]{1,0:T(8,128)}, /*index=5*/f32[128,128]{1,0:T(8,128)}) custom-call(bf16[32,16,128]{2,1,0:T(8,128)(2,1)S(1)} %get-tuple-element.12.refs_0_, bf16[32,16,128]{2,1,0:T(8,128)(2,1)S(1)} %get-tuple-element.13.refs_1_, ...), custom_call_target="tpu_custom_call" | custom-call | tf_op jit(solution)/shard_map/deliver/pallas_call | solution.py:504
